TPU v7x, 32 devices: a whole 2x2x4 slice. The times are simulated.
32 devices in a mesh: wire: 16 (over z, y, x), col: 2 (over core).
Axes of the slice: x: 2, y: 2, z: 4, core: 2. Of those that a mesh axis runs over, the one named last changes fastest.
Arguments:
- hamiltonian: bfloat16 [256, 3, 128, 128], P('wire')
- offsets: int32 [256, 3], P('wire'), may hold values from -2 to 2, as said below
- phase_left: bfloat16 [32768, 2048], P('wire'), may hold values from -0.125 to 0.125
- phase_right: bfloat16 [32768, 2048], P('wire'), may hold values from -0.03125 to 0.03125
- orbitals: bfloat16 [32768, 512], P('wire', 'col'), may hold values from -6 to 6
Outputs:
- gradient: float32 [32768, 512], P('wire', 'col')
Inputs may be any that keep to these rules, and one draw needn't show every extreme that they name: `offsets`: slot 0 of every row block has offset 0.
All inputs are finite; a program needn't handle non-finite values.
Results may differ from a plain program's by a relative error of at most 0.0017.
Values may be sent and summed in bfloat16 or wider, within the bound.
No kernel may reach another device: no remote copies, remote signals or barrier semaphores. Data moves between devices by JAX's collectives and lax.ppermute only.
A program may use at most 128 MiB of HBM per device.

v0:
```python
import math

import jax
import jax.numpy as jnp
from jax import lax
from jax.experimental import pallas as pl
from jax.experimental.layout import Layout, with_layout_constraint
from jax.experimental.pallas import tpu as pltpu
from jax.sharding import PartitionSpec as P


REACH = 2
F32 = jnp.float32
BF16 = jnp.bfloat16
F16 = jnp.float16


def split(value):
    high = lax.reduce_precision(value, 8, 7)
    return high.astype(BF16), (value - high).astype(BF16)


def dot(a, b):
    return jnp.dot(a, b, preferred_element_type=F32)


def dot_t(a, b):
    return lax.dot_general(a, b, (((0,), (0,)), ((), ())), preferred_element_type=F32)


def row_major(value):
    return with_layout_constraint(value, Layout(tuple(range(value.ndim))))


def band_kernel(picks_ref, core_ref, h_ref, x_ref, fetched_ref, swapped_ref, band_ref, pair_ref, tiles):
    blocks, slots, size, _ = h_ref.shape
    cols = x_ref.shape[1]
    reach = (tiles.shape[0] - blocks) // 2

    def put(at, ref, start, count):
        for k in range(count):
            tiles[at + k] = ref[start + k * size : start + (k + 1) * size]

    @pl.when(core_ref[0] == 0)
    def _():
        put(0, fetched_ref, 0, reach)
        put(reach + blocks, swapped_ref, 0, reach)

    @pl.when(core_ref[0] != 0)
    def _():
        put(0, swapped_ref, 0, reach)
        put(reach + blocks, fetched_ref, 0, reach)

    put(reach, x_ref, 0, blocks)

    @pl.loop(0, blocks, unroll=4)
    def _(j):
        total = dot(
            jnp.concatenate([h_ref[j, s] for s in range(slots)], axis=1),
            jnp.concatenate([tiles[picks_ref[j, s]] for s in range(slots)], axis=0),
        )
        rows = pl.ds(pl.multiple_of(j * size, size), size)
        high = total.astype(BF16)
        band_ref[rows, :] = total
        pair_ref[rows, :cols] = high
        pair_ref[rows, cols:] = (total - high.astype(F32)).astype(BF16)


def band_product(picks, core, hamiltonian, x, fetched, swapped):
    blocks, slots, size, _ = hamiltonian.shape
    rows, cols = x.shape
    vmem = pl.BlockSpec(memory_space=pltpu.VMEM)
    smem = pl.BlockSpec(memory_space=pltpu.SMEM)
    return pl.pallas_call(
        band_kernel,
        in_specs=[smem, smem, vmem, vmem, vmem, vmem],
        out_specs=[vmem, vmem],
        out_shape=[
            jax.ShapeDtypeStruct((rows, cols), F32),
            jax.ShapeDtypeStruct((rows, 2 * cols), BF16),
        ],
        scratch_shapes=[pltpu.VMEM((blocks + 2 * REACH, size, cols), BF16)],
        cost_estimate=pl.CostEstimate(
            flops=2 * slots * rows * size * cols, bytes_accessed=8 * rows * cols, transcendentals=0
        ),
        name="band",
    )(picks, core, hamiltonian, x, fetched, swapped)


class Cube:
    def __init__(self, chips, cores, orders):
        self.count = chips.bit_length() - 1
        me = lax.axis_index("wire")
        core = lax.axis_index("col") & 1
        self.perms = []
        self.bits = []
        for first, second in zip(*orders):
            axes = (first, second)
            self.perms.append(
                [
                    (w * cores + c, (w ^ (1 << axes[c & 1])) * cores + c)
                    for w in range(chips)
                    for c in range(cores)
                ]
            )
            self.bits.append((me >> jnp.where(core == 0, first, second)) & 1)

    def send(self, value, k):
        return lax.ppermute(value, ("wire", "col"), self.perms[k])

    def half(self, value, k, mine, axis=0):
        rows = value.shape[axis] // 2
        bit = self.bits[k] if mine else 1 - self.bits[k]
        return lax.dynamic_slice_in_dim(value, bit * rows, rows, axis)

    def reduce(self, value, got, start, wire_type, halved):
        for k in range(start, self.count):
            if k < halved:
                out = self.half(value, k, False)
                if got is not None:
                    out = out + self.half(got, k, False).astype(F32)
                out = out.astype(wire_type)
                value, got, out = lax.optimization_barrier((value, got, out))
                value = self.half(value, k, True)
                if got is not None:
                    value = value + self.half(got, k, True).astype(F32)
            else:
                if got is not None:
                    value = value + got.astype(F32)
                out = value.astype(wire_type)
            got = self.send(out, k)
        return value + got.astype(F32)

    def joined(self, value, got, k):
        return jnp.where(
            self.bits[k] == 0,
            jnp.concatenate([value, got], axis=0),
            jnp.concatenate([got, value], axis=0),
        )

    def gather(self, value, halved):
        for k in reversed(range(halved)):
            value = self.joined(value, self.send(value, k), k)
        return value


def steps(hamiltonian, offsets, phase_left, phase_right, orbitals):
    local_blocks = hamiltonian.shape[0]
    block_size = hamiltonian.shape[2]
    local_rows, cols = orbitals.shape
    rank = phase_left.shape[1]
    chips = lax.axis_size("wire")
    cores = lax.axis_size("col")
    total_rows = local_rows * chips
    count = chips.bit_length() - 1
    straight = list(range(count))
    crossed = list(range(count))
    first = list(straight)
    if count >= 3:
        first[1], first[2] = 2, 1
    if count >= 2:
        crossed[0], crossed[1] = 1, 0
    cube = Cube(chips, cores, (first, crossed))
    late = list(crossed)
    if count >= 4:
        late[2], late[3] = 3, 2
    small = Cube(chips, cores, (straight, late))
    swap = [(i, (i + 1) % cores) for i in range(cores)]

    scale = 2.0 ** -max(0, math.ceil(math.log2(36.0 * total_rows / 32768.0)))
    other = lax.ppermute(orbitals, "col", swap)

    def part(mine):
        right = cube.half(phase_right, 0, mine, axis=1)
        left = jnp.where((cube.bits[0] == 0) == mine, orbitals, other)
        return dot_t(right, orbitals), dot_t(left, orbitals) * scale

    away = jnp.concatenate([z.astype(F16) for z in part(False)], axis=0)
    got = cube.send(away, 0)
    here = jnp.concatenate(part(True), axis=0)
    halved = count - 1
    mine = cube.reduce(here, got, 1, F16, halved)

    width = REACH * block_size
    core = lax.axis_index("col") & 1
    ring = []
    for w in range(chips):
        for c in range(cores):
            ring.append((w * cores + c, (w + 1 - 2 * (c & 1)) % chips * cores + c))
    edge = jnp.concatenate(
        [
            jnp.where(core == 0, z[local_rows - width :], z[:width])
            for z in (orbitals, other)
        ],
        axis=0,
    )
    fetched = lax.ppermute(edge, ("wire", "col"), ring)
    swapped = lax.ppermute(fetched[width:], "col", swap)
    own_late, other_late, _ = lax.optimization_barrier((orbitals, other, away))
    both = jnp.concatenate([own_late, other_late], axis=1)
    offsets_late, _ = lax.optimization_barrier((offsets, away))
    picks = jnp.arange(local_blocks, dtype=jnp.int32)[:, None] + offsets_late + REACH
    band, pair = band_product(picks, core[None], hamiltonian, orbitals, fetched, swapped)
    cross_band = dot_t(both, pair)
    cross_band = cross_band[:, :cols] + cross_band[:, cols:]
    half_rank = rank // 2
    left_scale = 2.0 ** -max(0, math.ceil(math.log2(0.75 * local_rows / 32768.0)))
    left_away = (dot_t(both, cube.half(phase_left, 0, False, axis=1)) * left_scale).astype(F16)
    left_got = cube.send(left_away, 0)
    left_here = lax.optimization_barrier(dot_t(both, cube.half(phase_left, 0, True, axis=1)))
    left = split(left_here + left_got.astype(F32) * (1.0 / left_scale))
    left_high, left_low = lax.optimization_barrier(left)

    start = jnp.int32(0)
    span = here.shape[0]
    for bit in cube.bits[1:halved]:
        span //= 2
        start = start + bit * span
    row = start + lax.broadcasted_iota(jnp.int32, (mine.shape[0], 1), 0)
    mine = jnp.where(row < half_rank, lax.reduce_precision(mine, 8, 7), mine).astype(F16)
    for k in reversed(range(1, halved)):
        mine = cube.joined(mine, cube.send(mine, k), k)
    factor = mine[:half_rank].astype(BF16)
    cross_part = cross_band + dot(left_high, factor) + dot(left_low, factor)
    got = cube.send(mine, 0)
    low, top = jnp.where(cube.bits[0] == 0, mine, got), jnp.where(cube.bits[0] == 0, got, mine)
    coupling = jnp.concatenate([low[:half_rank], top[:half_rank]], axis=0).astype(BF16)
    inter = [z[half_rank:].astype(F32) * (1.0 / (scale * total_rows)) for z in (low, top)]

    halved = min(2, count)
    cross = small.gather(small.reduce(cross_part, None, 0, F32, halved), halved)
    cross = cross * (1.0 / total_rows)

    half_rows = local_rows // 2
    pieces = [slice(k * half_rows, (k + 1) * half_rows) for k in range(2)]
    image = []
    image_other = []
    factor = coupling
    for rows_k in pieces:
        pair_k = split(band[rows_k] + dot(phase_left[rows_k], factor))
        *pair_k, factor = lax.optimization_barrier((*pair_k, factor))
        image.append(pair_k)
    for value in image:
        image_other.append([lax.ppermute(z, "col", swap) for z in value])
    eye = (lax.broadcasted_iota(jnp.int32, (cols, cols), 0) == lax.broadcasted_iota(jnp.int32, (cols, cols), 1))
    weights = [split(w) for w in (2.0 * eye.astype(F32) - inter[0], -inter[1])]

    def weighed(value, weight):
        return dot(value[0], weight[0]) + dot(value[1], weight[0]) + dot(value[0], weight[1])

    base = [weighed(z, weights[0]) for z in image]
    base = [z + weighed(o, weights[1]) for z, o in zip(base, image_other)]
    high, low = split(cross)
    base = jnp.concatenate(base, axis=0)
    return row_major(base - (dot(both, high) + dot(both, low)))


def solution(mesh):
    return jax.shard_map(
        steps,
        mesh=mesh,
        in_specs=(
            P("wire", None, None, None),
            P("wire", None),
            P("wire", None),
            P("wire", None),
            P("wire", "col"),
        ),
        out_specs=P("wire", "col"),
        check_vma=False,
    )
```

profile of v0, /device:TPU:0, one launch (start us, length us, event | category | flops | bytes accessed | tf_op | source)
XLA Modules:
  0.0 116.0 jit_solution(16426071676542049043)
XLA Ops:
  0.0 0.5 collective-permute-start
  0.5 1.1 slice_select_fusion.1
  1.7 4.3 %fusion.8 = f32[1024,256]{1,0:T(8,128)S(1)} fusion(bf16[2048,256]{1,0:T(8,128)(2,1)} %x_ref.1, bf16[2048,2048]{1,0:T(8,128)(2,1)} %param.8, s32[]{:T(128)S(6)} %select_n.140), kind=kOutput, calls=%fused_computation.8 | convolution fusion | flops 1073741824 | bytes 6291460 | tf_op jit(solution)/shard_map/dot_general | solution.py:28
  6.0 1.3 %fusion.31 = f16[1024,256]{1,0:T(8,128)(2,1)S(1)} fusion(bf16[2048,256]{1,0:T(8,128)(2,1)S(1)} %copy-done, bf16[2048,2048]{1,0:T(8,128)(2,1)S(1)} %copy-done.6, s32[]{:T(128)S(6)} %select_n.129), kind=kOutput, calls=%fused_computation.42 | convolution fusion | flops 1074003968 | bytes 5767172 | tf_op jit(solution)/shard_map/dot_general | solution.py:28
  7.4 0.5 fusion.40
  8.3 2.5 %collective-permute-start.3 = (f16[1280,256]{1,0:T(8,128)(2,1)S(1)}, f16[1280,256]{1,0:T(8,128)(2,1)S(1)}, u32[]{:S(2)}, u32[]{:S(2)}) collective-permute-start(f16[1280,256]{1,0:T(8,128)(2,1)S(1)} %pad_maximum_fusion.1), channel_id=1, source_target_pairs={{0,2},{1,5},{2,0},{3,7},{4,6},{5,1},{6,4},{7,3},{8,10},{9,13},{10,... | collective-permute-start | bytes 1966088 | tf_op jit(solution)/shard_map/ppermute | solution.py:109
  10.9 1.1 copy-done.2
  12.1 0.7 pad_maximum_fusion.2
  12.9 0.5 fusion.37
  13.5 8.7 %collective-permute-done.3 = f16[1280,256]{1,0:T(8,128)(2,1)S(1)} collective-permute-done((f16[1280,256]{1,0:T(8,128)(2,1)S(1)}, f16[1280,256]{1,0:T(8,128)(2,1)S(1)}, u32[]{:S(2)}, u32[]{:S(2)}) %collective-permute-start.3) | collective-permute-done | bytes 655392 | tf_op jit(solution)/shard_map/ppermute | solution.py:109
  22.4 2.2 %collective-permute-start.4 = (f16[640,256]{1,0:T(8,128)(2,1)S(1)}, f16[640,256]{1,0:T(8,128)(2,1)S(1)}, u32[]{:S(2)}, u32[]{:S(2)}) collective-permute-start(f16[640,256]{1,0:T(8,128)(2,1)S(1)} %fusion.49), channel_id=1, source_target_pairs={{0,8},{1,3},{2,10},{3,1},{4,12},{5,7},{6,14},{7,5},{8,0},{9,11},{1... | collective-permute-start | bytes 983048 | tf_op jit(solution)/shard_map/ppermute | solution.py:109
  24.6 3.8 %fusion.2 = f32[512,1024]{1,0:T(8,128)} fusion(bf16[2048,512]{1,0:T(8,128)(2,1)S(1)} %constant_dynamic-update-slice_fusion, bf16[2048,2048]{1,0:T(8,128)(2,1)S(1)} %bitcast.31, s32[]{:T(128)S(6)} %select_n.140), kind=kOutput, calls=%fused_computation.2 | convolution fusion | flops 2147483648 | bytes 8388612 | tf_op jit(solution)/shard_map/dot_general | solution.py:28
  28.5 1.2 %collective-permute-done.4 = f16[640,256]{1,0:T(8,128)(2,1)S(1)} collective-permute-done((f16[640,256]{1,0:T(8,128)(2,1)S(1)}, f16[640,256]{1,0:T(8,128)(2,1)S(1)}, u32[]{:S(2)}, u32[]{:S(2)}) %collective-permute-start.4) | collective-permute-done | bytes 327712 | tf_op jit(solution)/shard_map/ppermute | solution.py:109
  29.7 0.7 add_convert_fusion
  30.4 6.3 %collective-permute-start.5 = (f16[320,256]{1,0:T(8,128)(2,1)}, f16[320,256]{1,0:T(8,128)(2,1)S(1)}, u32[]{:S(2)}, u32[]{:S(2)}) collective-permute-start(f16[320,256]{1,0:T(8,128)(2,1)} %add_convert_fusion), channel_id=1, source_target_pairs={{0,4},{1,9},{2,6},{3,11},{4,0},{5,13},{6,2},{7,15},{8,12},{9,1},{1... | collective-permute-start | bytes 491528 | tf_op jit(solution)/shard_map/ppermute | solution.py:109
  36.7 3.5 %fusion.18 = f16[512,1024]{1,0:T(8,128)(2,1)} fusion(bf16[2048,512]{1,0:T(8,128)(2,1)S(1)} %constant_dynamic-update-slice_fusion, bf16[2048,2048]{1,0:T(8,128)(2,1)S(1)} %bitcast.31, s32[]{:T(128)S(6)} %select_n.129), kind=kOutput, calls=%fused_computation.28 | convolution fusion | flops 2148007936 | bytes 7340036 | tf_op jit(solution)/shard_map/dot_general | solution.py:28
  40.3 1.6 %collective-permute-done.5 = f16[320,256]{1,0:T(8,128)(2,1)S(1)} collective-permute-done((f16[320,256]{1,0:T(8,128)(2,1)}, f16[320,256]{1,0:T(8,128)(2,1)S(1)}, u32[]{:S(2)}, u32[]{:S(2)}) %collective-permute-start.5) | collective-permute-done | bytes 163872 | tf_op jit(solution)/shard_map/ppermute | solution.py:109
  41.9 0.7 fusion.63
  42.7 2.6 %collective-permute-start.6 = (f16[320,256]{1,0:T(8,128)(2,1)}, f16[320,256]{1,0:T(8,128)(2,1)}, u32[]{:S(2)}, u32[]{:S(2)}) collective-permute-start(f16[320,256]{1,0:T(8,128)(2,1)} %fusion.63), channel_id=1, source_target_pairs={{0,16},{1,17},{2,18},{3,19},{4,20},{5,21},{6,22},{7,23},{8,24},{9,... | collective-permute-start | bytes 491528 | tf_op jit(solution)/shard_map/ppermute | solution.py:109
  45.3 0.6 add_add_fusion.1.picks_ref
  45.9 5.3 %band.1 = (f32[2048,256]{1,0:T(8,128)}, bf16[2048,512]{1,0:T(8,128)(2,1)}) custom-call(s32[16,3]{1,0:T(8,128)} %add_add_fusion.1.picks_ref, s32[1]{0:T(128)} %bitcast.core_ref, bf16[16,3,128,128]{3,2,1,0:T(8,128)(2,1)} %h_ref.1, bf16[2048,256]{1,0:T(8,128)(2,1)} %x_ref.1, bf16[512,256]{1,0:T(8,128)(2,1)} %copy-done.4, ...), custom_call_target="tpu_custom_call" | custom-call | flops 402653184 | bytes 4194304 | tf_op jit(solution)/shard_map/band/pallas_call | solution.py:74
  51.2 1.2 collective-permute-done.6
  52.4 1.0 fusion.54
  53.4 0.9 collective-permute-start.7
  54.4 3.0 %fusion.90 = f32[512,512]{1,0:T(8,128)S(1)} fusion(bf16[2048,512]{1,0:T(8,128)(2,1)S(1)} %constant_dynamic-update-slice_fusion, bf16[2048,512]{1,0:T(8,128)(2,1)} %get-tuple-element.43), kind=kOutput, calls=%fused_computation.125 | convolution fusion | flops 1073741824 | bytes 5242880 | tf_op jit(solution)/shard_map/dot_general | solution.py:28
  57.4 1.4 %collective-permute-done.7 = f16[320,256]{1,0:T(8,128)(2,1)S(1)} collective-permute-done((f16[320,256]{1,0:T(8,128)(2,1)S(1)}, f16[320,256]{1,0:T(8,128)(2,1)S(1)}, u32[]{:S(2)}, u32[]{:S(2)}) %collective-permute-start.7) | collective-permute-done | bytes 163872 | tf_op jit(solution)/shard_map/ppermute | solution.py:109
  59.0 0.8 collective-permute-start.8
  59.8 1.8 %fusion.13 = (bf16[512,1024]{1,0:T(8,128)(2,1)S(1)}, bf16[512,1024]{1,0:T(8,128)(2,1)S(1)}) fusion(f32[512,1024]{1,0:T(8,128)S(1)} %copy-done.3, f16[512,1024]{1,0:T(8,128)(2,1)} %collective-permute-done.14), kind=kLoop, calls=%fused_computation.16 | loop fusion | flops 3145728 | bytes 5242880 | tf_op jit(solution)/shard_map/convert_element_type | solution.py:20
  61.5 4.6 %collective-permute-done.8 = f16[640,256]{1,0:T(8,128)(2,1)S(1)} collective-permute-done((f16[640,256]{1,0:T(8,128)(2,1)S(1)}, f16[640,256]{1,0:T(8,128)(2,1)S(1)}, u32[]{:S(2)}, u32[]{:S(2)}) %collective-permute-start.8) | collective-permute-done | bytes 327712 | tf_op jit(solution)/shard_map/ppermute | solution.py:109
  66.4 0.4 fusion.53
  66.9 0.5 convolution_add_fusion.7
  67.3 0.7 constant_dynamic-slice_fusion.1
  68.1 2.0 %collective-permute-start.15 = (f32[256,256]{1,0:T(8,128)}, f32[256,256]{1,0:T(8,128)}, u32[]{:S(2)}, u32[]{:S(2)}) collective-permute-start(f32[256,256]{1,0:T(8,128)} %constant_dynamic-slice_fusion.1), channel_id=1, source_target_pairs={{0,2},{1,5},{2,0},{3,7},{4,6},{5,1},{6,4},{7,3},{8,10},{9,13},{10,... | collective-permute-start | bytes 786440 | tf_op jit(solution)/shard_map/ppermute | solution.py:109
  70.1 4.6 %collective-permute-done.15 = f32[256,256]{1,0:T(8,128)} collective-permute-done((f32[256,256]{1,0:T(8,128)}, f32[256,256]{1,0:T(8,128)}, u32[]{:S(2)}, u32[]{:S(2)}) %collective-permute-start.15) | collective-permute-done | bytes 262176 | tf_op jit(solution)/shard_map/ppermute | solution.py:109
  74.7 1.6 %dynamic-slice_add_fusion = f32[128,256]{1,0:T(8,128)} fusion(f32[256,256]{1,0:T(8,128)} %collective-permute-done.15, s32[]{:T(128)S(6)} %select_n.157, f32[512,256]{1,0:T(8,128)S(1)} %convolution_add_fusion.7, s32[]{:T(128)S(6)} %dynamic_slice.71), kind=kLoop, calls=%fused_computation.94 | loop fusion | flops 32768 | bytes 393224 | tf_op jit(solution)/shard_map/add | solution.py:121
  76.3 0.9 collective-permute-start.16
  77.2 4.3 %collective-permute-done.16 = f32[128,256]{1,0:T(8,128)S(1)} collective-permute-done((f32[128,256]{1,0:T(8,128)}, f32[128,256]{1,0:T(8,128)S(1)}, u32[]{:S(2)}, u32[]{:S(2)}) %collective-permute-start.16) | collective-permute-done | bytes 131104 | tf_op jit(solution)/shard_map/ppermute | solution.py:109
  81.5 0.9 add_add_fusion
  82.4 0.8 collective-permute-start.17
  83.2 4.4 %collective-permute-done.17 = f32[128,256]{1,0:T(8,128)S(1)} collective-permute-done((f32[128,256]{1,0:T(8,128)S(1)}, f32[128,256]{1,0:T(8,128)S(1)}, u32[]{:S(2)}, u32[]{:S(2)}) %collective-permute-start.17) | collective-permute-done | bytes 131104 | tf_op jit(solution)/shard_map/ppermute | solution.py:109
  87.6 2.4 %collective-permute-start.18 = (f32[128,256]{1,0:T(8,128)S(1)}, f32[128,256]{1,0:T(8,128)S(1)}, u32[]{:S(2)}, u32[]{:S(2)}) collective-permute-start(f32[128,256]{1,0:T(8,128)S(1)} %add.194), channel_id=1, source_target_pairs={{0,16},{1,9},{2,18},{3,11},{4,20},{5,13},{6,22},{7,15},{8,24},{9,1... | collective-permute-start | bytes 393224 | tf_op jit(solution)/shard_map/ppermute | solution.py:109
  90.1 1.4 %broadcast_select_fusion.1 = (f16[1280,256]{1,0:T(8,128)(2,1)S(1)}, f16[1280,256]{1,0:T(8,128)(2,1)S(1)}) fusion(f16[1280,256]{1,0:T(8,128)(2,1)S(1)} %maximum_select_fusion, f16[1280,256]{1,0:T(8,128)(2,1)} %collective-permute-done.9, pred[]{:T(512)S(6)} %eq.15), kind=kLoop, calls=%fused_computation.63 | loop fusion | flops 655360 | bytes 2621441 | tf_op jit(solution)/shard_map/jit(_where)/select_n | solution.py:226
  91.9 1.2 copy-done.7
  93.0 3.7 %fusion.43 = (bf16[1024,256]{1,0:T(8,128)(2,1)S(1)}, bf16[1024,256]{1,0:T(8,128)(2,1)S(1)}) fusion(f32[2048,256]{1,0:T(8,128)S(1)} %copy-done.7, f16[1024,256]{1,0:T(8,128)(2,1)S(1)} %slice.68, f16[1024,256]{1,0:T(8,128)(2,1)S(1)} %slice.67, bf16[2048,2048]{1,0:T(8,128)(2,1)} %param.7), kind=kOutput, calls=%fused_computation.47 | convolution fusion | flops 1076101120 | bytes 7340032 | tf_op jit(solution)/shard_map/dot_general | solution.py:24
  97.0 1.3 %fusion.44 = (bf16[1024,256]{1,0:T(8,128)(2,1)S(1)}, bf16[1024,256]{1,0:T(8,128)(2,1)S(1)}) fusion(f32[2048,256]{1,0:T(8,128)S(1)} %copy-done.7, bf16[2048,256]{1,0:T(8,128)(2,1)S(1)} %maximum_convert_fusion, bf16[2048,2048]{1,0:T(8,128)(2,1)S(1)} %bitcast.33), kind=kOutput, calls=%fused_computation.48 | convolution fusion | flops 1075052544 | bytes 7340032 | tf_op jit(solution)/shard_map/dot_general | solution.py:24
  98.2 0.3 fusion.88
  98.6 0.3 fusion.89
  98.9 0.6 collective-permute-start.10
  99.5 0.4 collective-permute-start.19
  99.9 1.2 %collective-permute-start.13 = (bf16[1024,256]{1,0:T(8,128)(2,1)S(1)}, bf16[1024,256]{1,0:T(8,128)(2,1)S(1)}, u32[]{:S(2)}, u32[]{:S(2)}) collective-permute-start(bf16[1024,256]{1,0:T(8,128)(2,1)S(1)} %get-tuple-element.40), channel_id=1, source_target_pairs={{0,1},{1,0},{2,3},{3,2},{4,5},{5,4},{6,7},{7,6},{8,9},{9,8},{10,11... | collective-permute-start | bytes 1572872 | tf_op jit(solution)/shard_map/ppermute | solution.py:244
  101.1 0.3 convolution_add_fusion.3
  101.4 0.3 convolution_add_fusion.2
  101.8 0.3 convolution_add_fusion.6
  102.1 2.4 %collective-permute-done.19 = f32[128,256]{1,0:T(8,128)S(1)} collective-permute-done((f32[128,256]{1,0:T(8,128)S(1)}, f32[128,256]{1,0:T(8,128)S(1)}, u32[]{:S(2)}, u32[]{:S(2)}) %collective-permute-start.19) | collective-permute-done | bytes 131104 | tf_op jit(solution)/shard_map/ppermute | solution.py:109
  104.6 1.8 %collective-permute-start.20 = (f32[256,256]{1,0:T(8,128)S(1)}, f32[256,256]{1,0:T(8,128)S(1)}, u32[]{:S(2)}, u32[]{:S(2)}) collective-permute-start(f32[256,256]{1,0:T(8,128)S(1)} %maximum_select_fusion.3), channel_id=1, source_target_pairs={{0,2},{1,5},{2,0},{3,7},{4,6},{5,1},{6,4},{7,3},{8,10},{9,13},{10,... | collective-permute-start | bytes 786440 | tf_op jit(solution)/shard_map/ppermute | solution.py:109
  106.4 0.3 convolution_add_fusion.5
  106.7 4.3 %collective-permute-done.20 = f32[256,256]{1,0:T(8,128)S(1)} collective-permute-done((f32[256,256]{1,0:T(8,128)S(1)}, f32[256,256]{1,0:T(8,128)S(1)}, u32[]{:S(2)}, u32[]{:S(2)}) %collective-permute-start.20) | collective-permute-done | bytes 262176 | tf_op jit(solution)/shard_map/ppermute | solution.py:109
  111.0 0.8 fusion.57
  111.8 0.3 fusion.64
  112.4 0.3 fusion.66
  112.7 0.3 fusion.87
  113.0 0.4 fusion.28
  113.4 0.4 fusion.30
  113.8 2.2 %fusion.12 = f32[2048,256]{1,0:T(8,128)} fusion(f32[2048,256]{1,0:T(8,128)S(1)} %fusion.57, bf16[2048,512]{1,0:T(8,128)(2,1)S(1)} %constant_dynamic-update-slice_fusion, f32[1024,256]{1,0:T(8,128)S(1)} %fusion.28, f32[1024,256]{1,0:T(8,128)S(1)} %fusion.30, f32[256,256]{1,0:T(8,128)S(1)} %maximum_select_fusion.3, ...), kind=kOutput, calls=%fused_computation.15 | convolution fusion | flops 539230208 | bytes 8912897 | tf_op jit(solution)/shard_map/dot_general | solution.py:24
  (60 shorter events, 2.9 us)
Async XLA Ops:
  0.0 7.4 %collective-permute-start = (bf16[2048,256]{1,0:T(8,128)(2,1)}, bf16[2048,256]{1,0:T(8,128)(2,1)S(1)}, u32[]{:S(2)}, u32[]{:S(2)}) collective-permute-start(bf16[2048,256]{1,0:T(8,128)(2,1)} %x_ref.1), channel_id=1, source_target_pairs={{0,1},{1,0},{2,3},{3,2},{4,5},{5,4},{6,7},{7,6},{8,9},{9,8},{10,11... | collective-permute-start | bytes 3145736 | tf_op jit(solution)/shard_map/ppermute | solution.py:171
  0.5 5.5 %copy-start.6 = (bf16[2048,2048]{1,0:T(8,128)(2,1)S(1)}, bf16[2048,2048]{1,0:T(8,128)(2,1)}, u32[]{:S(2)}) copy-start(bf16[2048,2048]{1,0:T(8,128)(2,1)} %param.8) | copy-start | bytes 25165828
  1.6 4.4 %copy-start = (bf16[2048,256]{1,0:T(8,128)(2,1)S(1)}, bf16[2048,256]{1,0:T(8,128)(2,1)}, u32[]{:S(2)}) copy-start(bf16[2048,256]{1,0:T(8,128)(2,1)} %x_ref.1) | copy-start | bytes 3145732
  1.7 23.0 %slice-start = ((s8[8388608]{0:T(1024)(128)(4,1)}), s8[4194304]{0:T(1024)(128)(4,1)S(1)}, s32[]{:S(2)}) async-start(s8[8388608]{0:T(1024)(128)(4,1)} %bitcast.30), calls=%async_computation | async-start | bytes 8388608
  6.0 18.6 %slice-start.1 = ((s8[8388608]{0:T(1024)(128)(4,1)}), s8[4194304]{0:T(1024)(128)(4,1)S(1)}, s32[]{:S(2)}) async-start(s8[8388608]{0:T(1024)(128)(4,1)} %bitcast.30), calls=%async_computation.1 | async-start | bytes 8388608
  7.4 1.0 copy-start.1
  8.3 13.8 %collective-permute-start.3 = (f16[1280,256]{1,0:T(8,128)(2,1)S(1)}, f16[1280,256]{1,0:T(8,128)(2,1)S(1)}, u32[]{:S(2)}, u32[]{:S(2)}) collective-permute-start(f16[1280,256]{1,0:T(8,128)(2,1)S(1)} %pad_maximum_fusion.1), channel_id=1, source_target_pairs={{0,2},{1,5},{2,0},{3,7},{4,6},{5,1},{6,4},{7,3},{8,10},{9,13},{10,... | collective-permute-start | bytes 1966088 | tf_op jit(solution)/shard_map/ppermute | solution.py:109
  10.8 1.2 %copy-start.2 = (bf16[2048,256]{1,0:T(8,128)(2,1)S(1)}, bf16[2048,256]{1,0:T(8,128)(2,1)}, u32[]{:S(2)}) copy-start(bf16[2048,256]{1,0:T(8,128)(2,1)} %copy-done.1) | copy-start | bytes 3145732
  12.8 27.4 %collective-permute-start.1 = (bf16[512,256]{1,0:T(8,128)(2,1)}, bf16[512,256]{1,0:T(8,128)(2,1)S(1)}, u32[]{:S(2)}, u32[]{:S(2)}) collective-permute-start(bf16[512,256]{1,0:T(8,128)(2,1)} %pad_maximum_fusion.2), channel_id=1, source_target_pairs={{0,2},{1,31},{2,4},{3,1},{4,6},{5,3},{6,8},{7,5},{8,10},{9,7},{10,... | collective-permute-start | bytes 786440 | tf_op jit(solution)/shard_map/ppermute | solution.py:197
  22.4 7.2 %collective-permute-start.4 = (f16[640,256]{1,0:T(8,128)(2,1)S(1)}, f16[640,256]{1,0:T(8,128)(2,1)S(1)}, u32[]{:S(2)}, u32[]{:S(2)}) collective-permute-start(f16[640,256]{1,0:T(8,128)(2,1)S(1)} %fusion.49), channel_id=1, source_target_pairs={{0,8},{1,3},{2,10},{3,1},{4,12},{5,7},{6,14},{7,5},{8,0},{9,11},{1... | collective-permute-start | bytes 983048 | tf_op jit(solution)/shard_map/ppermute | solution.py:109
  30.4 9.7 %copy-start.5 = (s32[16,3]{0,1:T(4,128)S(1)}, s32[16,3]{0,1:T(4,128)}, u32[]{:S(2)}) copy-start(s32[16,3]{0,1:T(4,128)} %param.6) | copy-start | bytes 580
  30.4 11.5 %collective-permute-start.5 = (f16[320,256]{1,0:T(8,128)(2,1)}, f16[320,256]{1,0:T(8,128)(2,1)S(1)}, u32[]{:S(2)}, u32[]{:S(2)}) collective-permute-start(f16[320,256]{1,0:T(8,128)(2,1)} %add_convert_fusion), channel_id=1, source_target_pairs={{0,4},{1,9},{2,6},{3,11},{4,0},{5,13},{6,2},{7,15},{8,12},{9,1},{1... | collective-permute-start | bytes 491528 | tf_op jit(solution)/shard_map/ppermute | solution.py:109
  40.1 19.6 %collective-permute-start.14 = (f16[512,1024]{1,0:T(8,128)(2,1)}, f16[512,1024]{1,0:T(8,128)(2,1)}, u32[]{:S(2)}, u32[]{:S(2)}) collective-permute-start(f16[512,1024]{1,0:T(8,128)(2,1)} %fusion.18), channel_id=1, source_target_pairs={{0,2},{1,5},{2,0},{3,7},{4,6},{5,1},{6,4},{7,3},{8,10},{9,13},{10,... | collective-permute-start | bytes 3145736 | tf_op jit(solution)/shard_map/ppermute | solution.py:109
  40.2 5.7 %copy-start.4 = (bf16[512,256]{1,0:T(8,128)(2,1)}, bf16[512,256]{1,0:T(8,128)(2,1)S(1)}, u32[]{:S(2)}) copy-start(bf16[512,256]{1,0:T(8,128)(2,1)S(1)} %collective-permute-done.1.fetched_ref) | copy-start | bytes 786436
  40.2 5.6 %collective-permute-start.2 = (bf16[256,256]{1,0:T(8,128)(2,1)S(1)}, bf16[256,256]{1,0:T(8,128)(2,1)}, u32[]{:S(2)}, u32[]{:S(2)}) collective-permute-start(bf16[256,256]{1,0:T(8,128)(2,1)S(1)} %slice.66), channel_id=1, source_target_pairs={{0,1},{1,0},{2,3},{3,2},{4,5},{5,4},{6,7},{7,6},{8,9},{9,8},{10,11... | collective-permute-start | bytes 393224 | tf_op jit(solution)/shard_map/ppermute | solution.py:198
  42.7 9.7 %collective-permute-start.6 = (f16[320,256]{1,0:T(8,128)(2,1)}, f16[320,256]{1,0:T(8,128)(2,1)}, u32[]{:S(2)}, u32[]{:S(2)}) collective-permute-start(f16[320,256]{1,0:T(8,128)(2,1)} %fusion.63), channel_id=1, source_target_pairs={{0,16},{1,17},{2,18},{3,19},{4,20},{5,21},{6,22},{7,23},{8,24},{9,... | collective-permute-start | bytes 491528 | tf_op jit(solution)/shard_map/ppermute | solution.py:109
  53.4 5.4 %collective-permute-start.7 = (f16[320,256]{1,0:T(8,128)(2,1)S(1)}, f16[320,256]{1,0:T(8,128)(2,1)S(1)}, u32[]{:S(2)}, u32[]{:S(2)}) collective-permute-start(f16[320,256]{1,0:T(8,128)(2,1)S(1)} %fusion.54), channel_id=1, source_target_pairs={{0,4},{1,9},{2,6},{3,11},{4,0},{5,13},{6,2},{7,15},{8,12},{9,1},{1... | collective-permute-start | bytes 491528 | tf_op jit(solution)/shard_map/ppermute | solution.py:109
  54.4 5.4 %copy-start.3 = (f32[512,1024]{1,0:T(8,128)S(1)}, f32[512,1024]{1,0:T(8,128)}, u32[]{:S(2)}) copy-start(f32[512,1024]{1,0:T(8,128)} %fusion.2) | copy-start | bytes 6291460
  59.0 7.1 %collective-permute-start.8 = (f16[640,256]{1,0:T(8,128)(2,1)S(1)}, f16[640,256]{1,0:T(8,128)(2,1)S(1)}, u32[]{:S(2)}, u32[]{:S(2)}) collective-permute-start(f16[640,256]{1,0:T(8,128)(2,1)S(1)} %maximum_select_fusion.2), channel_id=1, source_target_pairs={{0,8},{1,3},{2,10},{3,1},{4,12},{5,7},{6,14},{7,5},{8,0},{9,11},{1... | collective-permute-start | bytes 983048 | tf_op jit(solution)/shard_map/ppermute | solution.py:109
  68.1 6.7 %collective-permute-start.15 = (f32[256,256]{1,0:T(8,128)}, f32[256,256]{1,0:T(8,128)}, u32[]{:S(2)}, u32[]{:S(2)}) collective-permute-start(f32[256,256]{1,0:T(8,128)} %constant_dynamic-slice_fusion.1), channel_id=1, source_target_pairs={{0,2},{1,5},{2,0},{3,7},{4,6},{5,1},{6,4},{7,3},{8,10},{9,13},{10,... | collective-permute-start | bytes 786440 | tf_op jit(solution)/shard_map/ppermute | solution.py:109
  70.1 20.0 %collective-permute-start.9 = (f16[1280,256]{1,0:T(8,128)(2,1)S(1)}, f16[1280,256]{1,0:T(8,128)(2,1)}, u32[]{:S(2)}, u32[]{:S(2)}) collective-permute-start(f16[1280,256]{1,0:T(8,128)(2,1)S(1)} %maximum_select_fusion), channel_id=1, source_target_pairs={{0,2},{1,5},{2,0},{3,7},{4,6},{5,1},{6,4},{7,3},{8,10},{9,13},{10,... | collective-permute-start | bytes 1966088 | tf_op jit(solution)/shard_map/ppermute | solution.py:109
  76.3 5.2 %collective-permute-start.16 = (f32[128,256]{1,0:T(8,128)}, f32[128,256]{1,0:T(8,128)S(1)}, u32[]{:S(2)}, u32[]{:S(2)}) collective-permute-start(f32[128,256]{1,0:T(8,128)} %dynamic-slice_add_fusion), channel_id=1, source_target_pairs={{0,4},{1,3},{2,6},{3,1},{4,0},{5,7},{6,2},{7,5},{8,12},{9,11},{10,... | collective-permute-start | bytes 393224 | tf_op jit(solution)/shard_map/ppermute | solution.py:109
  82.4 5.2 %collective-permute-start.17 = (f32[128,256]{1,0:T(8,128)S(1)}, f32[128,256]{1,0:T(8,128)S(1)}, u32[]{:S(2)}, u32[]{:S(2)}) collective-permute-start(f32[128,256]{1,0:T(8,128)S(1)} %add_add_fusion), channel_id=1, source_target_pairs={{0,8},{1,17},{2,10},{3,19},{4,12},{5,21},{6,14},{7,23},{8,0},{9,25... | collective-permute-start | bytes 393224 | tf_op jit(solution)/shard_map/ppermute | solution.py:109
  87.6 11.8 %collective-permute-start.18 = (f32[128,256]{1,0:T(8,128)S(1)}, f32[128,256]{1,0:T(8,128)S(1)}, u32[]{:S(2)}, u32[]{:S(2)}) collective-permute-start(f32[128,256]{1,0:T(8,128)S(1)} %add.194), channel_id=1, source_target_pairs={{0,16},{1,9},{2,18},{3,11},{4,20},{5,13},{6,22},{7,15},{8,24},{9,1... | collective-permute-start | bytes 393224 | tf_op jit(solution)/shard_map/ppermute | solution.py:109
  91.4 1.6 %copy-start.7 = (f32[2048,256]{1,0:T(8,128)S(1)}, f32[2048,256]{1,0:T(8,128)}, u32[]{:S(2)}) copy-start(f32[2048,256]{1,0:T(8,128)} %get-tuple-element.29) | copy-start | bytes 6291460
  91.7 5.1 %slice-start.2 = ((s8[8388608]{0:T(1024)(128)(4,1)}), s8[4194304]{0:T(1024)(128)(4,1)S(1)}, s32[]{:S(2)}) async-start(s8[8388608]{0:T(1024)(128)(4,1)} %bitcast.32), calls=%async_computation.2 | async-start | bytes 8388608
  93.0 3.9 %slice-start.3 = ((s8[8388608]{0:T(1024)(128)(4,1)}), s8[4194304]{0:T(1024)(128)(4,1)S(1)}, s32[]{:S(2)}) async-start(s8[8388608]{0:T(1024)(128)(4,1)} %bitcast.32), calls=%async_computation.3 | async-start | bytes 8388608
  98.5 13.2 %collective-permute-start.12 = (bf16[1024,256]{1,0:T(8,128)(2,1)S(1)}, bf16[1024,256]{1,0:T(8,128)(2,1)S(1)}, u32[]{:S(2)}, u32[]{:S(2)}) collective-permute-start(bf16[1024,256]{1,0:T(8,128)(2,1)S(1)} %get-tuple-element.39), channel_id=1, source_target_pairs={{0,1},{1,0},{2,3},{3,2},{4,5},{5,4},{6,7},{7,6},{8,9},{9,8},{10,11... | collective-permute-start | bytes 1572872 | tf_op jit(solution)/shard_map/ppermute | solution.py:244
  98.9 13.5 %collective-permute-start.10 = (bf16[1024,256]{1,0:T(8,128)(2,1)S(1)}, bf16[1024,256]{1,0:T(8,128)(2,1)S(1)}, u32[]{:S(2)}, u32[]{:S(2)}) collective-permute-start(bf16[1024,256]{1,0:T(8,128)(2,1)S(1)} %get-tuple-element.36), channel_id=1, source_target_pairs={{0,1},{1,0},{2,3},{3,2},{4,5},{5,4},{6,7},{7,6},{8,9},{9,8},{10,11... | collective-permute-start | bytes 1572872 | tf_op jit(solution)/shard_map/ppermute | solution.py:244
  99.5 5.0 %collective-permute-start.19 = (f32[128,256]{1,0:T(8,128)S(1)}, f32[128,256]{1,0:T(8,128)S(1)}, u32[]{:S(2)}, u32[]{:S(2)}) collective-permute-start(f32[128,256]{1,0:T(8,128)S(1)} %add.195), channel_id=1, source_target_pairs={{0,4},{1,3},{2,6},{3,1},{4,0},{5,7},{6,2},{7,5},{8,12},{9,11},{10,... | collective-permute-start | bytes 393224 | tf_op jit(solution)/shard_map/ppermute | solution.py:109
  99.9 12.2 %collective-permute-start.13 = (bf16[1024,256]{1,0:T(8,128)(2,1)S(1)}, bf16[1024,256]{1,0:T(8,128)(2,1)S(1)}, u32[]{:S(2)}, u32[]{:S(2)}) collective-permute-start(bf16[1024,256]{1,0:T(8,128)(2,1)S(1)} %get-tuple-element.40), channel_id=1, source_target_pairs={{0,1},{1,0},{2,3},{3,2},{4,5},{5,4},{6,7},{7,6},{8,9},{9,8},{10,11... | collective-permute-start | bytes 1572872 | tf_op jit(solution)/shard_map/ppermute | solution.py:244
  101.7 10.9 %collective-permute-start.11 = (bf16[1024,256]{1,0:T(8,128)(2,1)S(1)}, bf16[1024,256]{1,0:T(8,128)(2,1)S(1)}, u32[]{:S(2)}, u32[]{:S(2)}) collective-permute-start(bf16[1024,256]{1,0:T(8,128)(2,1)S(1)} %get-tuple-element.37), channel_id=1, source_target_pairs={{0,1},{1,0},{2,3},{3,2},{4,5},{5,4},{6,7},{7,6},{8,9},{9,8},{10,11... | collective-permute-start | bytes 1572872 | tf_op jit(solution)/shard_map/ppermute | solution.py:244
  104.6 6.4 %collective-permute-start.20 = (f32[256,256]{1,0:T(8,128)S(1)}, f32[256,256]{1,0:T(8,128)S(1)}, u32[]{:S(2)}, u32[]{:S(2)}) collective-permute-start(f32[256,256]{1,0:T(8,128)S(1)} %maximum_select_fusion.3), channel_id=1, source_target_pairs={{0,2},{1,5},{2,0},{3,7},{4,6},{5,1},{6,4},{7,3},{8,10},{9,13},{10,... | collective-permute-start | bytes 786440 | tf_op jit(solution)/shard_map/ppermute | solution.py:109
where the time goes:
time: 116 us
  waiting for transfers between devices  38.8 us (33%)
  matrix products  29.6 us (26%)
  starting transfers between devices  26.1 us (22%)
  other arithmetic  11.9 us (10%)
  Pallas kernels  5.33 us (5%)
  local copies, waits for them, and re-layouts  4.02 us (3%)
    ppermute x14, waiting for transfers between devices, send(): return lax.ppermute(value, ('wire', 'col'), self.perms[k])  38.7 us
    ppermute x14, starting transfers between devices, send(): return lax.ppermute(value, ('wire', 'col'), self.perms[k])  23.6 us
    dot_general x7, matrix products, dot_t(): lax.dot_general(a, b, (((0,), (0,)), ((), ())), preferred_element_type=F32)  16.9 us
    dot_general x18, matrix products, dot(): return jnp.dot(a, b, preferred_element_type=F32)  12.7 us
    pallas_call x1, Pallas kernels, band_product(): pl.pallas_call(band_kernel, in_specs=[smem, smem, vmem, vmem, vmem, vmem]...  5.33 us
    unnamed x25, local copies, waits for them, and re-layouts  2.89 us
  transfers between devices with their start and end apart: 21, of which 11 were waited for; matrix products, arithmetic and copies ran while one was open for 32% of the time, Pallas kernels for 5%

commit v1 on v0

--- a/solution.py
+++ b/solution.py
@@ -222,36 +222,33 @@
         mine = cube.joined(mine, cube.send(mine, k), k)
     factor = mine[:half_rank].astype(BF16)
     cross_part = cross_band + dot(left_high, factor) + dot(left_low, factor)
+    image = band + dot(cube.half(phase_left, 0, True, axis=1), factor)
     got = cube.send(mine, 0)
-    low, top = jnp.where(cube.bits[0] == 0, mine, got), jnp.where(cube.bits[0] == 0, got, mine)
-    coupling = jnp.concatenate([low[:half_rank], top[:half_rank]], axis=0).astype(BF16)
-    inter = [z[half_rank:].astype(F32) * (1.0 / (scale * total_rows)) for z in (low, top)]
+    lower = cube.bits[0] == 0
+    inter = [
+        z.astype(F32) * (1.0 / (scale * total_rows))
+        for z in (
+            jnp.where(lower, mine[half_rank:], got[half_rank:]),
+            jnp.where(lower, got[half_rank:], mine[half_rank:]),
+        )
+    ]
 
     halved = min(2, count)
     cross = small.gather(small.reduce(cross_part, None, 0, F32, halved), halved)
     cross = cross * (1.0 / total_rows)
 
-    half_rows = local_rows // 2
-    pieces = [slice(k * half_rows, (k + 1) * half_rows) for k in range(2)]
-    image = []
-    image_other = []
-    factor = coupling
-    for rows_k in pieces:
-        pair_k = split(band[rows_k] + dot(phase_left[rows_k], factor))
-        *pair_k, factor = lax.optimization_barrier((*pair_k, factor))
-        image.append(pair_k)
-    for value in image:
-        image_other.append([lax.ppermute(z, "col", swap) for z in value])
+    factor = got[:half_rank].astype(BF16)
+    image = split(image + dot(cube.half(phase_left, 0, False, axis=1), factor))
+    image_other = [lax.ppermute(z, "col", swap) for z in image]
     eye = (lax.broadcasted_iota(jnp.int32, (cols, cols), 0) == lax.broadcasted_iota(jnp.int32, (cols, cols), 1))
     weights = [split(w) for w in (2.0 * eye.astype(F32) - inter[0], -inter[1])]
 
     def weighed(value, weight):
         return dot(value[0], weight[0]) + dot(value[1], weight[0]) + dot(value[0], weight[1])
 
-    base = [weighed(z, weights[0]) for z in image]
-    base = [z + weighed(o, weights[1]) for z, o in zip(base, image_other)]
+    base = weighed(image, weights[0])
+    base = base + weighed(image_other, weights[1])
     high, low = split(cross)
-    base = jnp.concatenate(base, axis=0)
     return row_major(base - (dot(both, high) + dot(both, low)))
 
 

time: 116 us -> 114 us (0.983)
  local copies, waits for them, and re-layouts: 4.02 us -> 1.42 us
    unnamed x25 -> x21, local copies, waits for them, and re-layouts: 2.89 us -> 0.51 us
    ppermute x14, starting transfers between devices: 23.6 us -> 25.3 us  [send(): return lax.ppermute(value, ('wire', 'col'), self.perms[k])]
    ppermute x4 -> x2, starting transfers between devices: 1.91 us -> 0.63 us  [steps(): image_other = [lax.ppermute(z, 'col', swap) for z in image]]
    dot_general x18 -> x12, matrix products: 12.7 us -> 13.8 us  [dot(): return jnp.dot(a, b, preferred_element_type=F32)]
  transfers between devices with their start and end apart: 21 -> 19, of which waited for: 11 -> 11; matrix products, arithmetic and copies ran while one was open for 32% -> 31% of each run, Pallas kernels for 5% -> 5%
where the time goes in v1:
time: 114 us
  waiting for transfers between devices  38 us (33%)
  matrix products  30.7 us (27%)
  starting transfers between devices  26.6 us (23%)
  other arithmetic  11.3 us (10%)
  Pallas kernels  5.38 us (5%)
  local copies, waits for them, and re-layouts  1.42 us (1%)
    ppermute x14, waiting for transfers between devices, send(): return lax.ppermute(value, ('wire', 'col'), self.perms[k])  38 us
    ppermute x14, starting transfers between devices, send(): return lax.ppermute(value, ('wire', 'col'), self.perms[k])  25.3 us
    dot_general x7, matrix products, dot_t(): lax.dot_general(a, b, (((0,), (0,)), ((), ())), preferred_element_type=F32)  16.9 us
    dot_general x12, matrix products, dot(): return jnp.dot(a, b, preferred_element_type=F32)  13.8 us
    pallas_call x1, Pallas kernels, band_product(): pl.pallas_call(band_kernel, in_specs=[smem, smem, vmem, vmem, vmem, vmem]...  5.38 us
  transfers between devices with their start and end apart: 19, of which 11 were waited for; matrix products, arithmetic and copies ran while one was open for 31% of the time, Pallas kernels for 5%

profile of v1, /device:TPU:0, one launch (start us, length us, event | category | flops | bytes accessed | tf_op | source)
XLA Modules:
  0.0 113.7 jit_solution(17784775304860158028)
XLA Ops:
  0.0 0.5 collective-permute-start
  0.5 1.1 slice_select_fusion.1
  1.7 4.3 %fusion = f32[1024,256]{1,0:T(8,128)S(1)} fusion(bf16[2048,256]{1,0:T(8,128)(2,1)} %x_ref.1, bf16[2048,2048]{1,0:T(8,128)(2,1)} %param.8, s32[]{:T(128)S(6)} %select_n.139), kind=kOutput, calls=%fused_computation | convolution fusion | flops 1073741824 | bytes 6291460 | tf_op jit(solution)/shard_map/dot_general | solution.py:28
  6.0 1.3 %fusion.24 = f16[1024,256]{1,0:T(8,128)(2,1)S(1)} fusion(bf16[2048,256]{1,0:T(8,128)(2,1)S(1)} %copy-done, bf16[2048,2048]{1,0:T(8,128)(2,1)S(1)} %copy-done.6, s32[]{:T(128)S(6)} %select_n.133), kind=kOutput, calls=%fused_computation.35 | convolution fusion | flops 1074003968 | bytes 5767172 | tf_op jit(solution)/shard_map/dot_general | solution.py:28
  7.4 0.5 fusion.33
  7.9 0.2 pad_maximum_fusion.1
  8.1 2.5 %collective-permute-start.3 = (f16[1280,256]{1,0:T(8,128)(2,1)S(1)}, f16[1280,256]{1,0:T(8,128)(2,1)S(1)}, u32[]{:S(2)}, u32[]{:S(2)}) collective-permute-start(f16[1280,256]{1,0:T(8,128)(2,1)S(1)} %pad_maximum_fusion.1), channel_id=1, source_target_pairs={{0,2},{1,5},{2,0},{3,7},{4,6},{5,1},{6,4},{7,3},{8,10},{9,13},{10,... | collective-permute-start | bytes 1966088 | tf_op jit(solution)/shard_map/ppermute | solution.py:109
  10.7 0.7 pad_maximum_fusion.2
  11.4 0.2 collective-permute-start.1
  11.7 0.3 copy-done.2
  12.1 0.5 fusion.30
  12.6 0.1 pad_maximum_fusion
  12.7 9.3 %collective-permute-done.3 = f16[1280,256]{1,0:T(8,128)(2,1)S(1)} collective-permute-done((f16[1280,256]{1,0:T(8,128)(2,1)S(1)}, f16[1280,256]{1,0:T(8,128)(2,1)S(1)}, u32[]{:S(2)}, u32[]{:S(2)}) %collective-permute-start.3) | collective-permute-done | bytes 655392 | tf_op jit(solution)/shard_map/ppermute | solution.py:109
  22.0 0.3 fusion.40
  22.3 2.2 %collective-permute-start.4 = (f16[640,256]{1,0:T(8,128)(2,1)S(1)}, f16[640,256]{1,0:T(8,128)(2,1)S(1)}, u32[]{:S(2)}, u32[]{:S(2)}) collective-permute-start(f16[640,256]{1,0:T(8,128)(2,1)S(1)} %fusion.40), channel_id=1, source_target_pairs={{0,8},{1,3},{2,10},{3,1},{4,12},{5,7},{6,14},{7,5},{8,0},{9,11},{1... | collective-permute-start | bytes 983048 | tf_op jit(solution)/shard_map/ppermute | solution.py:109
  24.5 3.8 %fusion.8 = f32[512,1024]{1,0:T(8,128)} fusion(bf16[2048,512]{1,0:T(8,128)(2,1)S(1)} %constant_dynamic-update-slice_fusion, bf16[2048,2048]{1,0:T(8,128)(2,1)S(1)} %bitcast.20, s32[]{:T(128)S(6)} %select_n.139), kind=kOutput, calls=%fused_computation.8 | convolution fusion | flops 2147483648 | bytes 8388612 | tf_op jit(solution)/shard_map/dot_general | solution.py:28
  28.3 1.2 %collective-permute-done.4 = f16[640,256]{1,0:T(8,128)(2,1)S(1)} collective-permute-done((f16[640,256]{1,0:T(8,128)(2,1)S(1)}, f16[640,256]{1,0:T(8,128)(2,1)S(1)}, u32[]{:S(2)}, u32[]{:S(2)}) %collective-permute-start.4) | collective-permute-done | bytes 327712 | tf_op jit(solution)/shard_map/ppermute | solution.py:109
  29.5 0.7 add_convert_fusion
  30.2 6.3 %collective-permute-start.5 = (f16[320,256]{1,0:T(8,128)(2,1)}, f16[320,256]{1,0:T(8,128)(2,1)S(1)}, u32[]{:S(2)}, u32[]{:S(2)}) collective-permute-start(f16[320,256]{1,0:T(8,128)(2,1)} %add_convert_fusion), channel_id=1, source_target_pairs={{0,4},{1,9},{2,6},{3,11},{4,0},{5,13},{6,2},{7,15},{8,12},{9,1},{1... | collective-permute-start | bytes 491528 | tf_op jit(solution)/shard_map/ppermute | solution.py:109
  36.5 3.4 %fusion.21 = f16[512,1024]{1,0:T(8,128)(2,1)} fusion(bf16[2048,512]{1,0:T(8,128)(2,1)S(1)} %constant_dynamic-update-slice_fusion, bf16[2048,2048]{1,0:T(8,128)(2,1)S(1)} %bitcast.20, s32[]{:T(128)S(6)} %select_n.133), kind=kOutput, calls=%fused_computation.33 | convolution fusion | flops 2148007936 | bytes 7340036 | tf_op jit(solution)/shard_map/dot_general | solution.py:28
  40.1 1.6 %collective-permute-done.5 = f16[320,256]{1,0:T(8,128)(2,1)S(1)} collective-permute-done((f16[320,256]{1,0:T(8,128)(2,1)}, f16[320,256]{1,0:T(8,128)(2,1)S(1)}, u32[]{:S(2)}, u32[]{:S(2)}) %collective-permute-start.5) | collective-permute-done | bytes 163872 | tf_op jit(solution)/shard_map/ppermute | solution.py:109
  41.8 0.7 fusion.63
  42.5 2.6 %collective-permute-start.6 = (f16[320,256]{1,0:T(8,128)(2,1)}, f16[320,256]{1,0:T(8,128)(2,1)}, u32[]{:S(2)}, u32[]{:S(2)}) collective-permute-start(f16[320,256]{1,0:T(8,128)(2,1)} %fusion.63), channel_id=1, source_target_pairs={{0,16},{1,17},{2,18},{3,19},{4,20},{5,21},{6,22},{7,23},{8,24},{9,... | collective-permute-start | bytes 491528 | tf_op jit(solution)/shard_map/ppermute | solution.py:109
  45.1 0.6 add_add_fusion.2.picks_ref
  45.7 5.4 %band.1 = (f32[2048,256]{1,0:T(8,128)}, bf16[2048,512]{1,0:T(8,128)(2,1)}) custom-call(s32[16,3]{1,0:T(8,128)} %add_add_fusion.2.picks_ref, s32[1]{0:T(128)} %bitcast.core_ref, bf16[16,3,128,128]{3,2,1,0:T(8,128)(2,1)} %h_ref.1, bf16[2048,256]{1,0:T(8,128)(2,1)} %x_ref.1, bf16[512,256]{1,0:T(8,128)(2,1)} %copy-done.4, ...), custom_call_target="tpu_custom_call" | custom-call | flops 402653184 | bytes 4194304 | tf_op jit(solution)/shard_map/band/pallas_call | solution.py:74
  51.1 1.1 collective-permute-done.6
  52.2 1.0 fusion.47
  53.3 1.0 collective-permute-start.7
  54.2 3.0 %fusion.88 = f32[512,512]{1,0:T(8,128)S(1)} fusion(bf16[2048,512]{1,0:T(8,128)(2,1)S(1)} %constant_dynamic-update-slice_fusion, bf16[2048,512]{1,0:T(8,128)(2,1)} %get-tuple-element.33), kind=kOutput, calls=%fused_computation.121 | convolution fusion | flops 1073741824 | bytes 5242880 | tf_op jit(solution)/shard_map/dot_general | solution.py:28
  57.2 1.4 %collective-permute-done.7 = f16[320,256]{1,0:T(8,128)(2,1)S(1)} collective-permute-done((f16[320,256]{1,0:T(8,128)(2,1)S(1)}, f16[320,256]{1,0:T(8,128)(2,1)S(1)}, u32[]{:S(2)}, u32[]{:S(2)}) %collective-permute-start.7) | collective-permute-done | bytes 163872 | tf_op jit(solution)/shard_map/ppermute | solution.py:109
  58.7 0.2 maximum_select_fusion.2
  58.8 0.7 collective-permute-start.8
  59.6 1.8 %fusion.16 = (bf16[512,1024]{1,0:T(8,128)(2,1)S(1)}, bf16[512,1024]{1,0:T(8,128)(2,1)S(1)}) fusion(f32[512,1024]{1,0:T(8,128)S(1)} %copy-done.3, f16[512,1024]{1,0:T(8,128)(2,1)} %collective-permute-done.12), kind=kLoop, calls=%fused_computation.24 | loop fusion | flops 3145728 | bytes 5242880 | tf_op jit(solution)/shard_map/convert_element_type | solution.py:20
  61.3 4.6 %collective-permute-done.8 = f16[640,256]{1,0:T(8,128)(2,1)S(1)} collective-permute-done((f16[640,256]{1,0:T(8,128)(2,1)S(1)}, f16[640,256]{1,0:T(8,128)(2,1)S(1)}, u32[]{:S(2)}, u32[]{:S(2)}) %collective-permute-start.8) | collective-permute-done | bytes 327712 | tf_op jit(solution)/shard_map/ppermute | solution.py:109
  66.0 0.3 maximum_select_fusion
  66.3 0.4 fusion.46
  66.7 0.4 convolution_add_fusion.4
  67.2 0.7 constant_dynamic-slice_fusion.1
  67.9 2.0 %collective-permute-start.13 = (f32[256,256]{1,0:T(8,128)}, f32[256,256]{1,0:T(8,128)}, u32[]{:S(2)}, u32[]{:S(2)}) collective-permute-start(f32[256,256]{1,0:T(8,128)} %constant_dynamic-slice_fusion.1), channel_id=1, source_target_pairs={{0,2},{1,5},{2,0},{3,7},{4,6},{5,1},{6,4},{7,3},{8,10},{9,13},{10,... | collective-permute-start | bytes 786440 | tf_op jit(solution)/shard_map/ppermute | solution.py:109
  69.9 4.7 %collective-permute-done.13 = f32[256,256]{1,0:T(8,128)} collective-permute-done((f32[256,256]{1,0:T(8,128)}, f32[256,256]{1,0:T(8,128)}, u32[]{:S(2)}, u32[]{:S(2)}) %collective-permute-start.13) | collective-permute-done | bytes 262176 | tf_op jit(solution)/shard_map/ppermute | solution.py:109
  74.6 1.6 %dynamic-slice_add_fusion = f32[128,256]{1,0:T(8,128)} fusion(f32[256,256]{1,0:T(8,128)} %collective-permute-done.13, s32[]{:T(128)S(6)} %select_n.161, f32[512,256]{1,0:T(8,128)S(1)} %convolution_add_fusion.4, s32[]{:T(128)S(6)} %dynamic_slice.73), kind=kLoop, calls=%fused_computation.82 | loop fusion | flops 32768 | bytes 393224 | tf_op jit(solution)/shard_map/add | solution.py:121
  76.1 0.9 collective-permute-start.14
  77.0 1.1 collective-permute-start.9
  78.1 4.6 %collective-permute-done.14 = f32[128,256]{1,0:T(8,128)S(1)} collective-permute-done((f32[128,256]{1,0:T(8,128)}, f32[128,256]{1,0:T(8,128)S(1)}, u32[]{:S(2)}, u32[]{:S(2)}) %collective-permute-start.14) | collective-permute-done | bytes 131104 | tf_op jit(solution)/shard_map/ppermute | solution.py:109
  82.7 0.9 add_add_fusion.1
  83.7 0.7 collective-permute-start.15
  84.4 3.4 %fusion.10 = f32[2048,256]{1,0:T(8,128)S(1)} fusion(bf16[2048,2048]{1,0:T(8,128)(2,1)} %param.7, s32[]{:T(128)S(6)} %select_n.139, f16[1280,256]{1,0:T(8,128)(2,1)S(1)} %maximum_select_fusion), kind=kOutput, calls=%fused_computation.10 | convolution fusion | flops 1074003968 | bytes 6815748 | tf_op jit(solution)/shard_map/dot_general | solution.py:24
  87.9 2.1 %collective-permute-done.15 = f32[128,256]{1,0:T(8,128)S(1)} collective-permute-done((f32[128,256]{1,0:T(8,128)S(1)}, f32[128,256]{1,0:T(8,128)S(1)}, u32[]{:S(2)}, u32[]{:S(2)}) %collective-permute-start.15) | collective-permute-done | bytes 131104 | tf_op jit(solution)/shard_map/ppermute | solution.py:109
  90.0 1.8 %collective-permute-start.16 = (f32[128,256]{1,0:T(8,128)S(1)}, f32[128,256]{1,0:T(8,128)S(1)}, u32[]{:S(2)}, u32[]{:S(2)}) collective-permute-start(f32[128,256]{1,0:T(8,128)S(1)} %add.176), channel_id=1, source_target_pairs={{0,16},{1,9},{2,18},{3,11},{4,20},{5,13},{6,22},{7,15},{8,24},{9,1... | collective-permute-start | bytes 393224 | tf_op jit(solution)/shard_map/ppermute | solution.py:109
  91.8 3.7 %fusion.15 = (bf16[2048,256]{1,0:T(8,128)(2,1)S(1)}, bf16[2048,256]{1,0:T(8,128)(2,1)S(1)}) fusion(f16[1280,256]{1,0:T(8,128)(2,1)} %collective-permute-done.9, bf16[2048,2048]{1,0:T(8,128)(2,1)} %param.7, s32[]{:T(128)S(6)} %select_n.133, f32[2048,256]{1,0:T(8,128)S(1)} %copy-done.7, f32[2048,256]{1,0:T(8,128)S(1)} %fusion.10), kind=kOutput, calls=%fused_computation.23 | convolution fusion | flops 1077149696 | bytes 11010052 | tf_op jit(solution)/shard_map/dot_general | solution.py:24
  95.5 1.0 broadcast_select_fusion
  96.5 0.4 fusion.65
  96.9 0.6 collective-permute-start.11
  97.5 1.1 collective-permute-start.17
  98.6 0.4 convolution_add_fusion.3
  99.1 3.5 %collective-permute-done.17 = f32[128,256]{1,0:T(8,128)S(1)} collective-permute-done((f32[128,256]{1,0:T(8,128)S(1)}, f32[128,256]{1,0:T(8,128)S(1)}, u32[]{:S(2)}, u32[]{:S(2)}) %collective-permute-start.17) | collective-permute-done | bytes 131104 | tf_op jit(solution)/shard_map/ppermute | solution.py:109
  102.6 2.3 %collective-permute-start.18 = (f32[256,256]{1,0:T(8,128)S(1)}, f32[256,256]{1,0:T(8,128)S(1)}, u32[]{:S(2)}, u32[]{:S(2)}) collective-permute-start(f32[256,256]{1,0:T(8,128)S(1)} %maximum_select_fusion.3), channel_id=1, source_target_pairs={{0,2},{1,5},{2,0},{3,7},{4,6},{5,1},{6,4},{7,3},{8,10},{9,13},{10,... | collective-permute-start | bytes 786440 | tf_op jit(solution)/shard_map/ppermute | solution.py:109
  104.9 0.5 convolution_add_fusion.2
  105.4 3.9 %collective-permute-done.18 = f32[256,256]{1,0:T(8,128)S(1)} collective-permute-done((f32[256,256]{1,0:T(8,128)S(1)}, f32[256,256]{1,0:T(8,128)S(1)}, u32[]{:S(2)}, u32[]{:S(2)}) %collective-permute-start.18) | collective-permute-done | bytes 262176 | tf_op jit(solution)/shard_map/ppermute | solution.py:109
  109.3 0.8 fusion.50
  110.0 0.4 fusion.56
  110.5 0.4 fusion.64
  110.9 0.7 fusion.14
  111.6 2.0 %fusion.12 = f32[2048,256]{1,0:T(8,128)} fusion(f32[2048,256]{1,0:T(8,128)S(1)} %fusion.14, f32[2048,256]{1,0:T(8,128)S(1)} %fusion.50, bf16[2048,512]{1,0:T(8,128)(2,1)S(1)} %constant_dynamic-update-slice_fusion, f32[256,256]{1,0:T(8,128)S(1)} %maximum_select_fusion.3, f32[256,256]{1,0:T(8,128)S(1)} %collective-permute-done.18, pred[]{:T(512)S(6)} %eq.15), kind=kOutput, calls=%fused_computation.17 | convolution fusion | flops 538705920 | bytes 8912897 | tf_op jit(solution)/shard_map/dot_general | solution.py:24
  (42 shorter events, 0.7 us)
Async XLA Ops:
  0.0 7.4 %collective-permute-start = (bf16[2048,256]{1,0:T(8,128)(2,1)}, bf16[2048,256]{1,0:T(8,128)(2,1)S(1)}, u32[]{:S(2)}, u32[]{:S(2)}) collective-permute-start(bf16[2048,256]{1,0:T(8,128)(2,1)} %x_ref.1), channel_id=1, source_target_pairs={{0,1},{1,0},{2,3},{3,2},{4,5},{5,4},{6,7},{7,6},{8,9},{9,8},{10,11... | collective-permute-start | bytes 3145736 | tf_op jit(solution)/shard_map/ppermute | solution.py:171
  0.5 5.5 %copy-start.6 = (bf16[2048,2048]{1,0:T(8,128)(2,1)S(1)}, bf16[2048,2048]{1,0:T(8,128)(2,1)}, u32[]{:S(2)}) copy-start(bf16[2048,2048]{1,0:T(8,128)(2,1)} %param.8) | copy-start | bytes 25165828
  1.6 4.4 %copy-start = (bf16[2048,256]{1,0:T(8,128)(2,1)S(1)}, bf16[2048,256]{1,0:T(8,128)(2,1)}, u32[]{:S(2)}) copy-start(bf16[2048,256]{1,0:T(8,128)(2,1)} %x_ref.1) | copy-start | bytes 3145732
  1.7 22.8 %slice-start = ((s8[8388608]{0:T(1024)(128)(4,1)}), s8[4194304]{0:T(1024)(128)(4,1)S(1)}, s32[]{:S(2)}) async-start(s8[8388608]{0:T(1024)(128)(4,1)} %bitcast.19), calls=%async_computation | async-start | bytes 8388608
  6.0 18.4 %slice-start.1 = ((s8[8388608]{0:T(1024)(128)(4,1)}), s8[4194304]{0:T(1024)(128)(4,1)S(1)}, s32[]{:S(2)}) async-start(s8[8388608]{0:T(1024)(128)(4,1)} %bitcast.19), calls=%async_computation.1 | async-start | bytes 8388608
  7.4 3.3 %copy-start.1 = (bf16[2048,256]{1,0:T(8,128)(2,1)}, bf16[2048,256]{1,0:T(8,128)(2,1)S(1)}, u32[]{:S(2)}) copy-start(bf16[2048,256]{1,0:T(8,128)(2,1)S(1)} %collective-permute-done) | copy-start | bytes 3145732
  8.1 13.9 %collective-permute-start.3 = (f16[1280,256]{1,0:T(8,128)(2,1)S(1)}, f16[1280,256]{1,0:T(8,128)(2,1)S(1)}, u32[]{:S(2)}, u32[]{:S(2)}) collective-permute-start(f16[1280,256]{1,0:T(8,128)(2,1)S(1)} %pad_maximum_fusion.1), channel_id=1, source_target_pairs={{0,2},{1,5},{2,0},{3,7},{4,6},{5,1},{6,4},{7,3},{8,10},{9,13},{10,... | collective-permute-start | bytes 1966088 | tf_op jit(solution)/shard_map/ppermute | solution.py:109
  10.7 1.3 %copy-start.2 = (bf16[2048,256]{1,0:T(8,128)(2,1)S(1)}, bf16[2048,256]{1,0:T(8,128)(2,1)}, u32[]{:S(2)}) copy-start(bf16[2048,256]{1,0:T(8,128)(2,1)} %copy-done.1) | copy-start | bytes 3145732
  11.4 28.6 %collective-permute-start.1 = (bf16[512,256]{1,0:T(8,128)(2,1)}, bf16[512,256]{1,0:T(8,128)(2,1)S(1)}, u32[]{:S(2)}, u32[]{:S(2)}) collective-permute-start(bf16[512,256]{1,0:T(8,128)(2,1)} %pad_maximum_fusion.2), channel_id=1, source_target_pairs={{0,2},{1,31},{2,4},{3,1},{4,6},{5,3},{6,8},{7,5},{8,10},{9,7},{10,... | collective-permute-start | bytes 786440 | tf_op jit(solution)/shard_map/ppermute | solution.py:197
  22.3 7.2 %collective-permute-start.4 = (f16[640,256]{1,0:T(8,128)(2,1)S(1)}, f16[640,256]{1,0:T(8,128)(2,1)S(1)}, u32[]{:S(2)}, u32[]{:S(2)}) collective-permute-start(f16[640,256]{1,0:T(8,128)(2,1)S(1)} %fusion.40), channel_id=1, source_target_pairs={{0,8},{1,3},{2,10},{3,1},{4,12},{5,7},{6,14},{7,5},{8,0},{9,11},{1... | collective-permute-start | bytes 983048 | tf_op jit(solution)/shard_map/ppermute | solution.py:109
  30.2 9.7 %copy-start.5 = (s32[16,3]{0,1:T(4,128)S(1)}, s32[16,3]{0,1:T(4,128)}, u32[]{:S(2)}) copy-start(s32[16,3]{0,1:T(4,128)} %param.6) | copy-start | bytes 580
  30.2 11.5 %collective-permute-start.5 = (f16[320,256]{1,0:T(8,128)(2,1)}, f16[320,256]{1,0:T(8,128)(2,1)S(1)}, u32[]{:S(2)}, u32[]{:S(2)}) collective-permute-start(f16[320,256]{1,0:T(8,128)(2,1)} %add_convert_fusion), channel_id=1, source_target_pairs={{0,4},{1,9},{2,6},{3,11},{4,0},{5,13},{6,2},{7,15},{8,12},{9,1},{1... | collective-permute-start | bytes 491528 | tf_op jit(solution)/shard_map/ppermute | solution.py:109
  40.0 19.5 %collective-permute-start.12 = (f16[512,1024]{1,0:T(8,128)(2,1)}, f16[512,1024]{1,0:T(8,128)(2,1)}, u32[]{:S(2)}, u32[]{:S(2)}) collective-permute-start(f16[512,1024]{1,0:T(8,128)(2,1)} %fusion.21), channel_id=1, source_target_pairs={{0,2},{1,5},{2,0},{3,7},{4,6},{5,1},{6,4},{7,3},{8,10},{9,13},{10,... | collective-permute-start | bytes 3145736 | tf_op jit(solution)/shard_map/ppermute | solution.py:109
  40.0 5.7 %copy-start.4 = (bf16[512,256]{1,0:T(8,128)(2,1)}, bf16[512,256]{1,0:T(8,128)(2,1)S(1)}, u32[]{:S(2)}) copy-start(bf16[512,256]{1,0:T(8,128)(2,1)S(1)} %collective-permute-done.1.fetched_ref) | copy-start | bytes 786436
  40.1 5.6 %collective-permute-start.2 = (bf16[256,256]{1,0:T(8,128)(2,1)S(1)}, bf16[256,256]{1,0:T(8,128)(2,1)}, u32[]{:S(2)}, u32[]{:S(2)}) collective-permute-start(bf16[256,256]{1,0:T(8,128)(2,1)S(1)} %slice.48), channel_id=1, source_target_pairs={{0,1},{1,0},{2,3},{3,2},{4,5},{5,4},{6,7},{7,6},{8,9},{9,8},{10,11... | collective-permute-start | bytes 393224 | tf_op jit(solution)/shard_map/ppermute | solution.py:198
  42.5 9.7 %collective-permute-start.6 = (f16[320,256]{1,0:T(8,128)(2,1)}, f16[320,256]{1,0:T(8,128)(2,1)}, u32[]{:S(2)}, u32[]{:S(2)}) collective-permute-start(f16[320,256]{1,0:T(8,128)(2,1)} %fusion.63), channel_id=1, source_target_pairs={{0,16},{1,17},{2,18},{3,19},{4,20},{5,21},{6,22},{7,23},{8,24},{9,... | collective-permute-start | bytes 491528 | tf_op jit(solution)/shard_map/ppermute | solution.py:109
  53.3 5.4 %collective-permute-start.7 = (f16[320,256]{1,0:T(8,128)(2,1)S(1)}, f16[320,256]{1,0:T(8,128)(2,1)S(1)}, u32[]{:S(2)}, u32[]{:S(2)}) collective-permute-start(f16[320,256]{1,0:T(8,128)(2,1)S(1)} %fusion.47), channel_id=1, source_target_pairs={{0,4},{1,9},{2,6},{3,11},{4,0},{5,13},{6,2},{7,15},{8,12},{9,1},{1... | collective-permute-start | bytes 491528 | tf_op jit(solution)/shard_map/ppermute | solution.py:109
  54.2 5.3 %copy-start.3 = (f32[512,1024]{1,0:T(8,128)S(1)}, f32[512,1024]{1,0:T(8,128)}, u32[]{:S(2)}) copy-start(f32[512,1024]{1,0:T(8,128)} %fusion.8) | copy-start | bytes 6291460
  58.8 7.1 %collective-permute-start.8 = (f16[640,256]{1,0:T(8,128)(2,1)S(1)}, f16[640,256]{1,0:T(8,128)(2,1)S(1)}, u32[]{:S(2)}, u32[]{:S(2)}) collective-permute-start(f16[640,256]{1,0:T(8,128)(2,1)S(1)} %maximum_select_fusion.2), channel_id=1, source_target_pairs={{0,8},{1,3},{2,10},{3,1},{4,12},{5,7},{6,14},{7,5},{8,0},{9,11},{1... | collective-permute-start | bytes 983048 | tf_op jit(solution)/shard_map/ppermute | solution.py:109
  67.9 6.7 %collective-permute-start.13 = (f32[256,256]{1,0:T(8,128)}, f32[256,256]{1,0:T(8,128)}, u32[]{:S(2)}, u32[]{:S(2)}) collective-permute-start(f32[256,256]{1,0:T(8,128)} %constant_dynamic-slice_fusion.1), channel_id=1, source_target_pairs={{0,2},{1,5},{2,0},{3,7},{4,6},{5,1},{6,4},{7,3},{8,10},{9,13},{10,... | collective-permute-start | bytes 786440 | tf_op jit(solution)/shard_map/ppermute | solution.py:109
  76.1 6.6 %collective-permute-start.14 = (f32[128,256]{1,0:T(8,128)}, f32[128,256]{1,0:T(8,128)S(1)}, u32[]{:S(2)}, u32[]{:S(2)}) collective-permute-start(f32[128,256]{1,0:T(8,128)} %dynamic-slice_add_fusion), channel_id=1, source_target_pairs={{0,4},{1,3},{2,6},{3,1},{4,0},{5,7},{6,2},{7,5},{8,12},{9,11},{10,... | collective-permute-start | bytes 393224 | tf_op jit(solution)/shard_map/ppermute | solution.py:109
  77.0 14.7 %collective-permute-start.9 = (f16[1280,256]{1,0:T(8,128)(2,1)S(1)}, f16[1280,256]{1,0:T(8,128)(2,1)}, u32[]{:S(2)}, u32[]{:S(2)}) collective-permute-start(f16[1280,256]{1,0:T(8,128)(2,1)S(1)} %maximum_select_fusion), channel_id=1, source_target_pairs={{0,2},{1,5},{2,0},{3,7},{4,6},{5,1},{6,4},{7,3},{8,10},{9,13},{10,... | collective-permute-start | bytes 1966088 | tf_op jit(solution)/shard_map/ppermute | solution.py:109
  83.6 8.1 %copy-start.7 = (f32[2048,256]{1,0:T(8,128)S(1)}, f32[2048,256]{1,0:T(8,128)}, u32[]{:S(2)}) copy-start(f32[2048,256]{1,0:T(8,128)} %get-tuple-element.24) | copy-start | bytes 6291460
  83.7 6.3 %collective-permute-start.15 = (f32[128,256]{1,0:T(8,128)S(1)}, f32[128,256]{1,0:T(8,128)S(1)}, u32[]{:S(2)}, u32[]{:S(2)}) collective-permute-start(f32[128,256]{1,0:T(8,128)S(1)} %add_add_fusion.1), channel_id=1, source_target_pairs={{0,8},{1,17},{2,10},{3,19},{4,12},{5,21},{6,14},{7,23},{8,0},{9,25... | collective-permute-start | bytes 393224 | tf_op jit(solution)/shard_map/ppermute | solution.py:109
  90.0 7.5 %collective-permute-start.16 = (f32[128,256]{1,0:T(8,128)S(1)}, f32[128,256]{1,0:T(8,128)S(1)}, u32[]{:S(2)}, u32[]{:S(2)}) collective-permute-start(f32[128,256]{1,0:T(8,128)S(1)} %add.176), channel_id=1, source_target_pairs={{0,16},{1,9},{2,18},{3,11},{4,20},{5,13},{6,22},{7,15},{8,24},{9,1... | collective-permute-start | bytes 393224 | tf_op jit(solution)/shard_map/ppermute | solution.py:109
  95.4 14.6 %collective-permute-start.10 = (bf16[2048,256]{1,0:T(8,128)(2,1)S(1)}, bf16[2048,256]{1,0:T(8,128)(2,1)S(1)}, u32[]{:S(2)}, u32[]{:S(2)}) collective-permute-start(bf16[2048,256]{1,0:T(8,128)(2,1)S(1)} %get-tuple-element.44), channel_id=1, source_target_pairs={{0,1},{1,0},{2,3},{3,2},{4,5},{5,4},{6,7},{7,6},{8,9},{9,8},{10,11... | collective-permute-start | bytes 3145736 | tf_op jit(solution)/shard_map/ppermute | solution.py:242
  96.9 13.5 %collective-permute-start.11 = (bf16[2048,256]{1,0:T(8,128)(2,1)S(1)}, bf16[2048,256]{1,0:T(8,128)(2,1)S(1)}, u32[]{:S(2)}, u32[]{:S(2)}) collective-permute-start(bf16[2048,256]{1,0:T(8,128)(2,1)S(1)} %get-tuple-element.43), channel_id=1, source_target_pairs={{0,1},{1,0},{2,3},{3,2},{4,5},{5,4},{6,7},{7,6},{8,9},{9,8},{10,11... | collective-permute-start | bytes 3145736 | tf_op jit(solution)/shard_map/ppermute | solution.py:242
  97.5 5.0 %collective-permute-start.17 = (f32[128,256]{1,0:T(8,128)S(1)}, f32[128,256]{1,0:T(8,128)S(1)}, u32[]{:S(2)}, u32[]{:S(2)}) collective-permute-start(f32[128,256]{1,0:T(8,128)S(1)} %add.177), channel_id=1, source_target_pairs={{0,4},{1,3},{2,6},{3,1},{4,0},{5,7},{6,2},{7,5},{8,12},{9,11},{10,... | collective-permute-start | bytes 393224 | tf_op jit(solution)/shard_map/ppermute | solution.py:109
  102.6 6.7 %collective-permute-start.18 = (f32[256,256]{1,0:T(8,128)S(1)}, f32[256,256]{1,0:T(8,128)S(1)}, u32[]{:S(2)}, u32[]{:S(2)}) collective-permute-start(f32[256,256]{1,0:T(8,128)S(1)} %maximum_select_fusion.3), channel_id=1, source_target_pairs={{0,2},{1,5},{2,0},{3,7},{4,6},{5,1},{6,4},{7,3},{8,10},{9,13},{10,... | collective-permute-start | bytes 786440 | tf_op jit(solution)/shard_map/ppermute | solution.py:109

commit v2 on v1

--- a/solution.py
+++ b/solution.py
@@ -222,7 +222,7 @@
         mine = cube.joined(mine, cube.send(mine, k), k)
     factor = mine[:half_rank].astype(BF16)
     cross_part = cross_band + dot(left_high, factor) + dot(left_low, factor)
-    image = band + dot(cube.half(phase_left, 0, True, axis=1), factor)
+    image = dot(cube.half(phase_left, 0, True, axis=1), factor)
     got = cube.send(mine, 0)
     lower = cube.bits[0] == 0
     inter = [
@@ -238,16 +238,30 @@
     cross = cross * (1.0 / total_rows)
 
     factor = got[:half_rank].astype(BF16)
-    image = split(image + dot(cube.half(phase_left, 0, False, axis=1), factor))
-    image_other = [lax.ppermute(z, "col", swap) for z in image]
+    half_rows = local_rows // 2
+    halves = []
+    halves_other = []
+    for k in range(2):
+        rows_left = lax.dynamic_slice(
+            phase_left,
+            (k * half_rows, (1 - cube.bits[0]) * half_rank),
+            (half_rows, half_rank),
+        )
+        span = slice(k * half_rows, (k + 1) * half_rows)
+        value = split(band[span] + image[span] + dot(rows_left, factor))
+        *value, factor = lax.optimization_barrier((*value, factor))
+        halves.append(value)
+    for value in halves:
+        halves_other.append([lax.ppermute(z, "col", swap) for z in value])
     eye = (lax.broadcasted_iota(jnp.int32, (cols, cols), 0) == lax.broadcasted_iota(jnp.int32, (cols, cols), 1))
     weights = [split(w) for w in (2.0 * eye.astype(F32) - inter[0], -inter[1])]
 
     def weighed(value, weight):
         return dot(value[0], weight[0]) + dot(value[1], weight[0]) + dot(value[0], weight[1])
 
-    base = weighed(image, weights[0])
-    base = base + weighed(image_other, weights[1])
+    base = [weighed(z, weights[0]) for z in halves]
+    base = [z + weighed(o, weights[1]) for z, o in zip(base, halves_other)]
+    base = jnp.concatenate(base, axis=0)
     high, low = split(cross)
     return row_major(base - (dot(both, high) + dot(both, low)))
 

time: 114 us -> 117 us (1.026)
  waiting for transfers between devices: 38 us -> 35.8 us
  matrix products: 30.7 us -> 32.8 us
    ppermute x14, waiting for transfers between devices: 38 us -> 35.8 us  [send(): return lax.ppermute(value, ('wire', 'col'), self.perms[k])]
    dot_general x12 -> x19, matrix products: 13.8 us -> 15.9 us  [dot(): return jnp.dot(a, b, preferred_element_type=F32)]
  transfers between devices with their start and end apart: 19 -> 21, of which waited for: 11 -> 11; matrix products, arithmetic and copies ran while one was open for 31% -> 33% of each run, Pallas kernels for 5% -> 5%
where the time goes in v2:
time: 117 us
  waiting for transfers between devices  35.8 us (31%)
  matrix products  32.8 us (28%)
  starting transfers between devices  27.6 us (24%)
  other arithmetic  12.4 us (11%)
  Pallas kernels  5.33 us (5%)
  local copies, waits for them, and re-layouts  2.47 us (2%)
    ppermute x14, waiting for transfers between devices, send(): return lax.ppermute(value, ('wire', 'col'), self.perms[k])  35.8 us
    ppermute x14, starting transfers between devices, send(): return lax.ppermute(value, ('wire', 'col'), self.perms[k])  25.3 us
    dot_general x7, matrix products, dot_t(): lax.dot_general(a, b, (((0,), (0,)), ((), ())), preferred_element_type=F32)  16.9 us
    dot_general x19, matrix products, dot(): return jnp.dot(a, b, preferred_element_type=F32)  15.9 us
    pallas_call x1, Pallas kernels, band_product(): pl.pallas_call(band_kernel, in_specs=[smem, smem, vmem, vmem, vmem, vmem]...  5.33 us
  transfers between devices with their start and end apart: 21, of which 11 were waited for; matrix products, arithmetic and copies ran while one was open for 33% of the time, Pallas kernels for 5%

profile of v2, /device:TPU:0, one launch (start us, length us, event | category | flops | bytes accessed | tf_op | source)
XLA Modules:
  0.0 116.8 jit_solution(5988017419778702887)
XLA Ops:
  0.0 0.5 collective-permute-start
  0.5 1.1 slice_select_fusion.1
  1.7 4.3 %fusion.2 = f32[1024,256]{1,0:T(8,128)S(1)} fusion(bf16[2048,256]{1,0:T(8,128)(2,1)} %x_ref.1, bf16[2048,2048]{1,0:T(8,128)(2,1)} %param.8, s32[]{:T(128)S(6)} %select_n.140), kind=kOutput, calls=%fused_computation.2 | convolution fusion | flops 1073741824 | bytes 6291460 | tf_op jit(solution)/shard_map/dot_general | solution.py:28
  6.0 1.3 %fusion.27 = f16[1024,256]{1,0:T(8,128)(2,1)S(1)} fusion(bf16[2048,256]{1,0:T(8,128)(2,1)S(1)} %copy-done, bf16[2048,2048]{1,0:T(8,128)(2,1)S(1)} %copy-done.7, s32[]{:T(128)S(6)} %select_n.134), kind=kOutput, calls=%fused_computation.42 | convolution fusion | flops 1074003968 | bytes 5767172 | tf_op jit(solution)/shard_map/dot_general | solution.py:28
  7.4 0.5 fusion.36
  8.3 2.5 %collective-permute-start.3 = (f16[1280,256]{1,0:T(8,128)(2,1)S(1)}, f16[1280,256]{1,0:T(8,128)(2,1)S(1)}, u32[]{:S(2)}, u32[]{:S(2)}) collective-permute-start(f16[1280,256]{1,0:T(8,128)(2,1)S(1)} %pad_maximum_fusion.1), channel_id=1, source_target_pairs={{0,2},{1,5},{2,0},{3,7},{4,6},{5,1},{6,4},{7,3},{8,10},{9,13},{10,... | collective-permute-start | bytes 1966088 | tf_op jit(solution)/shard_map/ppermute | solution.py:109
  10.9 1.1 copy-done.2
  12.1 0.7 pad_maximum_fusion.2
  12.9 0.5 fusion.33
  13.5 8.7 %collective-permute-done.3 = f16[1280,256]{1,0:T(8,128)(2,1)S(1)} collective-permute-done((f16[1280,256]{1,0:T(8,128)(2,1)S(1)}, f16[1280,256]{1,0:T(8,128)(2,1)S(1)}, u32[]{:S(2)}, u32[]{:S(2)}) %collective-permute-start.3) | collective-permute-done | bytes 655392 | tf_op jit(solution)/shard_map/ppermute | solution.py:109
  22.4 2.2 %collective-permute-start.4 = (f16[640,256]{1,0:T(8,128)(2,1)S(1)}, f16[640,256]{1,0:T(8,128)(2,1)S(1)}, u32[]{:S(2)}, u32[]{:S(2)}) collective-permute-start(f16[640,256]{1,0:T(8,128)(2,1)S(1)} %fusion.47), channel_id=1, source_target_pairs={{0,8},{1,3},{2,10},{3,1},{4,12},{5,7},{6,14},{7,5},{8,0},{9,11},{1... | collective-permute-start | bytes 983048 | tf_op jit(solution)/shard_map/ppermute | solution.py:109
  24.6 3.8 %fusion.6 = f32[512,1024]{1,0:T(8,128)} fusion(bf16[2048,512]{1,0:T(8,128)(2,1)S(1)} %constant_dynamic-update-slice_fusion, bf16[2048,2048]{1,0:T(8,128)(2,1)S(1)} %bitcast.27, s32[]{:T(128)S(6)} %select_n.140), kind=kOutput, calls=%fused_computation.6 | convolution fusion | flops 2147483648 | bytes 8388612 | tf_op jit(solution)/shard_map/dot_general | solution.py:28
  28.5 1.2 %collective-permute-done.4 = f16[640,256]{1,0:T(8,128)(2,1)S(1)} collective-permute-done((f16[640,256]{1,0:T(8,128)(2,1)S(1)}, f16[640,256]{1,0:T(8,128)(2,1)S(1)}, u32[]{:S(2)}, u32[]{:S(2)}) %collective-permute-start.4) | collective-permute-done | bytes 327712 | tf_op jit(solution)/shard_map/ppermute | solution.py:109
  29.7 0.7 add_convert_fusion
  30.4 6.3 %collective-permute-start.5 = (f16[320,256]{1,0:T(8,128)(2,1)}, f16[320,256]{1,0:T(8,128)(2,1)S(1)}, u32[]{:S(2)}, u32[]{:S(2)}) collective-permute-start(f16[320,256]{1,0:T(8,128)(2,1)} %add_convert_fusion), channel_id=1, source_target_pairs={{0,4},{1,9},{2,6},{3,11},{4,0},{5,13},{6,2},{7,15},{8,12},{9,1},{1... | collective-permute-start | bytes 491528 | tf_op jit(solution)/shard_map/ppermute | solution.py:109
  36.7 3.5 %fusion.20 = f16[512,1024]{1,0:T(8,128)(2,1)} fusion(bf16[2048,512]{1,0:T(8,128)(2,1)S(1)} %constant_dynamic-update-slice_fusion, bf16[2048,2048]{1,0:T(8,128)(2,1)S(1)} %bitcast.27, s32[]{:T(128)S(6)} %select_n.134), kind=kOutput, calls=%fused_computation.30 | convolution fusion | flops 2148007936 | bytes 7340036 | tf_op jit(solution)/shard_map/dot_general | solution.py:28
  40.3 1.6 %collective-permute-done.5 = f16[320,256]{1,0:T(8,128)(2,1)S(1)} collective-permute-done((f16[320,256]{1,0:T(8,128)(2,1)}, f16[320,256]{1,0:T(8,128)(2,1)S(1)}, u32[]{:S(2)}, u32[]{:S(2)}) %collective-permute-start.5) | collective-permute-done | bytes 163872 | tf_op jit(solution)/shard_map/ppermute | solution.py:109
  41.9 0.7 fusion.61
  42.7 2.6 %collective-permute-start.6 = (f16[320,256]{1,0:T(8,128)(2,1)}, f16[320,256]{1,0:T(8,128)(2,1)}, u32[]{:S(2)}, u32[]{:S(2)}) collective-permute-start(f16[320,256]{1,0:T(8,128)(2,1)} %fusion.61), channel_id=1, source_target_pairs={{0,16},{1,17},{2,18},{3,19},{4,20},{5,21},{6,22},{7,23},{8,24},{9,... | collective-permute-start | bytes 491528 | tf_op jit(solution)/shard_map/ppermute | solution.py:109
  45.3 0.6 add_add_fusion.1.picks_ref
  45.9 5.3 %band.1 = (f32[2048,256]{1,0:T(8,128)}, bf16[2048,512]{1,0:T(8,128)(2,1)}) custom-call(s32[16,3]{1,0:T(8,128)} %add_add_fusion.1.picks_ref, s32[1]{0:T(128)} %bitcast.core_ref, bf16[16,3,128,128]{3,2,1,0:T(8,128)(2,1)} %h_ref.1, bf16[2048,256]{1,0:T(8,128)(2,1)} %x_ref.1, bf16[512,256]{1,0:T(8,128)(2,1)} %copy-done.5, ...), custom_call_target="tpu_custom_call" | custom-call | flops 402653184 | bytes 4194304 | tf_op jit(solution)/shard_map/band/pallas_call | solution.py:74
  51.2 1.2 collective-permute-done.6
  52.4 1.0 fusion.52
  53.4 0.9 collective-permute-start.7
  54.4 3.0 %fusion.95 = f32[512,512]{1,0:T(8,128)S(1)} fusion(bf16[2048,512]{1,0:T(8,128)(2,1)S(1)} %constant_dynamic-update-slice_fusion, bf16[2048,512]{1,0:T(8,128)(2,1)} %get-tuple-element.43), kind=kOutput, calls=%fused_computation.130 | convolution fusion | flops 1073741824 | bytes 5242880 | tf_op jit(solution)/shard_map/dot_general | solution.py:28
  57.4 1.4 %collective-permute-done.7 = f16[320,256]{1,0:T(8,128)(2,1)S(1)} collective-permute-done((f16[320,256]{1,0:T(8,128)(2,1)S(1)}, f16[320,256]{1,0:T(8,128)(2,1)S(1)}, u32[]{:S(2)}, u32[]{:S(2)}) %collective-permute-start.7) | collective-permute-done | bytes 163872 | tf_op jit(solution)/shard_map/ppermute | solution.py:109
  59.0 0.8 collective-permute-start.8
  59.8 1.8 %fusion.11 = (bf16[512,1024]{1,0:T(8,128)(2,1)S(1)}, bf16[512,1024]{1,0:T(8,128)(2,1)S(1)}) fusion(f32[512,1024]{1,0:T(8,128)S(1)} %copy-done.3, f16[512,1024]{1,0:T(8,128)(2,1)} %collective-permute-done.14), kind=kLoop, calls=%fused_computation.14 | loop fusion | flops 3145728 | bytes 5242880 | tf_op jit(solution)/shard_map/convert_element_type | solution.py:20
  61.5 4.6 %collective-permute-done.8 = f16[640,256]{1,0:T(8,128)(2,1)S(1)} collective-permute-done((f16[640,256]{1,0:T(8,128)(2,1)S(1)}, f16[640,256]{1,0:T(8,128)(2,1)S(1)}, u32[]{:S(2)}, u32[]{:S(2)}) %collective-permute-start.8) | collective-permute-done | bytes 327712 | tf_op jit(solution)/shard_map/ppermute | solution.py:109
  66.4 0.4 fusion.51
  66.9 0.4 convolution_add_fusion.7
  67.3 0.7 constant_dynamic-slice_fusion.1
  68.1 2.0 %collective-permute-start.15 = (f32[256,256]{1,0:T(8,128)}, f32[256,256]{1,0:T(8,128)}, u32[]{:S(2)}, u32[]{:S(2)}) collective-permute-start(f32[256,256]{1,0:T(8,128)} %constant_dynamic-slice_fusion.1), channel_id=1, source_target_pairs={{0,2},{1,5},{2,0},{3,7},{4,6},{5,1},{6,4},{7,3},{8,10},{9,13},{10,... | collective-permute-start | bytes 786440 | tf_op jit(solution)/shard_map/ppermute | solution.py:109
  70.1 4.6 %collective-permute-done.15 = f32[256,256]{1,0:T(8,128)} collective-permute-done((f32[256,256]{1,0:T(8,128)}, f32[256,256]{1,0:T(8,128)}, u32[]{:S(2)}, u32[]{:S(2)}) %collective-permute-start.15) | collective-permute-done | bytes 262176 | tf_op jit(solution)/shard_map/ppermute | solution.py:109
  74.7 1.6 %dynamic-slice_add_fusion = f32[128,256]{1,0:T(8,128)} fusion(f32[256,256]{1,0:T(8,128)} %collective-permute-done.15, s32[]{:T(128)S(6)} %select_n.162, f32[512,256]{1,0:T(8,128)S(1)} %convolution_add_fusion.7, s32[]{:T(128)S(6)} %dynamic_slice.80), kind=kLoop, calls=%fused_computation.94 | loop fusion | flops 32768 | bytes 393224 | tf_op jit(solution)/shard_map/add | solution.py:121
  76.3 0.9 collective-permute-start.16
  77.2 1.2 collective-permute-start.9
  78.4 4.5 %collective-permute-done.16 = f32[128,256]{1,0:T(8,128)S(1)} collective-permute-done((f32[128,256]{1,0:T(8,128)}, f32[128,256]{1,0:T(8,128)S(1)}, u32[]{:S(2)}, u32[]{:S(2)}) %collective-permute-start.16) | collective-permute-done | bytes 131104 | tf_op jit(solution)/shard_map/ppermute | solution.py:109
  82.9 0.9 add_add_fusion
  83.8 0.8 collective-permute-start.17
  84.6 3.5 %fusion.8 = f32[2048,256]{1,0:T(8,128)S(1)} fusion(bf16[2048,2048]{1,0:T(8,128)(2,1)} %param.7, s32[]{:T(128)S(6)} %select_n.140, f16[1280,256]{1,0:T(8,128)(2,1)S(1)} %maximum_select_fusion), kind=kOutput, calls=%fused_computation.8 | convolution fusion | flops 1074003968 | bytes 6815748 | tf_op jit(solution)/shard_map/dot_general | solution.py:24
  88.1 2.0 %collective-permute-done.17 = f32[128,256]{1,0:T(8,128)S(1)} collective-permute-done((f32[128,256]{1,0:T(8,128)S(1)}, f32[128,256]{1,0:T(8,128)S(1)}, u32[]{:S(2)}, u32[]{:S(2)}) %collective-permute-start.17) | collective-permute-done | bytes 131104 | tf_op jit(solution)/shard_map/ppermute | solution.py:109
  90.1 1.8 %collective-permute-start.18 = (f32[128,256]{1,0:T(8,128)S(1)}, f32[128,256]{1,0:T(8,128)S(1)}, u32[]{:S(2)}, u32[]{:S(2)}) collective-permute-start(f32[128,256]{1,0:T(8,128)S(1)} %add.205), channel_id=1, source_target_pairs={{0,16},{1,9},{2,18},{3,11},{4,20},{5,13},{6,22},{7,15},{8,24},{9,1... | collective-permute-start | bytes 393224 | tf_op jit(solution)/shard_map/ppermute | solution.py:109
  91.9 1.1 slice_convert_fusion
  93.1 2.4 %fusion.39 = (bf16[1024,256]{1,0:T(8,128)(2,1)S(1)}, bf16[1024,256]{1,0:T(8,128)(2,1)S(1)}) fusion(f16[1280,256]{1,0:T(8,128)(2,1)} %collective-permute-done.9, bf16[2048,2048]{1,0:T(8,128)(2,1)} %param.7, s32[]{:T(128)S(6)} %select_n.134, f32[2048,256]{1,0:T(8,128)S(1)} %fusion.8, f32[2048,256]{1,0:T(8,128)S(1)} %copy-done.4), kind=kOutput, calls=%fused_computation.47 | convolution fusion | flops 538705920 | bytes 5767172 | tf_op jit(solution)/shard_map/dot_general | solution.py:24
  95.5 2.3 %fusion.40 = (bf16[1024,256]{1,0:T(8,128)(2,1)S(1)}, bf16[1024,256]{1,0:T(8,128)(2,1)S(1)}) fusion(bf16[1024,256]{1,0:T(8,128)(2,1)S(1)} %slice_convert_fusion, bf16[2048,2048]{1,0:T(8,128)(2,1)} %param.7, s32[]{:T(128)S(6)} %select_n.134, f32[2048,256]{1,0:T(8,128)S(1)} %fusion.8, f32[2048,256]{1,0:T(8,128)S(1)} %copy-done.4), kind=kOutput, calls=%fused_computation.48 | convolution fusion | flops 538443776 | bytes 5767172 | tf_op jit(solution)/shard_map/dot_general | solution.py:24
  97.9 1.0 broadcast_select_fusion
  98.9 0.3 fusion.93
  99.2 0.3 fusion.94
  99.5 0.6 collective-permute-start.10
  100.1 1.1 collective-permute-start.19
  101.1 1.0 collective-permute-start.13
  102.2 0.3 convolution_add_fusion.3
  102.5 0.3 convolution_add_fusion.2
  102.9 0.3 convolution_add_fusion.6
  103.2 1.9 %collective-permute-done.19 = f32[128,256]{1,0:T(8,128)S(1)} collective-permute-done((f32[128,256]{1,0:T(8,128)S(1)}, f32[128,256]{1,0:T(8,128)S(1)}, u32[]{:S(2)}, u32[]{:S(2)}) %collective-permute-start.19) | collective-permute-done | bytes 131104 | tf_op jit(solution)/shard_map/ppermute | solution.py:109
  105.1 2.4 %collective-permute-start.20 = (f32[256,256]{1,0:T(8,128)S(1)}, f32[256,256]{1,0:T(8,128)S(1)}, u32[]{:S(2)}, u32[]{:S(2)}) collective-permute-start(f32[256,256]{1,0:T(8,128)S(1)} %maximum_select_fusion.3), channel_id=1, source_target_pairs={{0,2},{1,5},{2,0},{3,7},{4,6},{5,1},{6,4},{7,3},{8,10},{9,13},{10,... | collective-permute-start | bytes 786440 | tf_op jit(solution)/shard_map/ppermute | solution.py:109
  107.5 0.3 convolution_add_fusion.5
  107.8 4.0 %collective-permute-done.20 = f32[256,256]{1,0:T(8,128)S(1)} collective-permute-done((f32[256,256]{1,0:T(8,128)S(1)}, f32[256,256]{1,0:T(8,128)S(1)}, u32[]{:S(2)}, u32[]{:S(2)}) %collective-permute-start.20) | collective-permute-done | bytes 262176 | tf_op jit(solution)/shard_map/ppermute | solution.py:109
  111.8 0.8 fusion.55
  112.6 0.3 fusion.62
  113.2 0.3 fusion.64
  113.9 0.4 fusion.24
  114.5 2.2 %fusion.10 = f32[2048,256]{1,0:T(8,128)} fusion(f32[2048,256]{1,0:T(8,128)S(1)} %fusion.55, bf16[2048,512]{1,0:T(8,128)(2,1)S(1)} %constant_dynamic-update-slice_fusion, f32[1024,256]{1,0:T(8,128)S(1)} %fusion.24, f32[1024,256]{1,0:T(8,128)S(1)} %fusion.26, f32[256,256]{1,0:T(8,128)S(1)} %maximum_select_fusion.3, ...), kind=kOutput, calls=%fused_computation.13 | convolution fusion | flops 539230208 | bytes 8912897 | tf_op jit(solution)/shard_map/dot_general | solution.py:24
  (54 shorter events, 2.9 us)
Async XLA Ops:
  0.0 7.4 %collective-permute-start = (bf16[2048,256]{1,0:T(8,128)(2,1)}, bf16[2048,256]{1,0:T(8,128)(2,1)S(1)}, u32[]{:S(2)}, u32[]{:S(2)}) collective-permute-start(bf16[2048,256]{1,0:T(8,128)(2,1)} %x_ref.1), channel_id=1, source_target_pairs={{0,1},{1,0},{2,3},{3,2},{4,5},{5,4},{6,7},{7,6},{8,9},{9,8},{10,11... | collective-permute-start | bytes 3145736 | tf_op jit(solution)/shard_map/ppermute | solution.py:171
  0.5 5.5 %copy-start.7 = (bf16[2048,2048]{1,0:T(8,128)(2,1)S(1)}, bf16[2048,2048]{1,0:T(8,128)(2,1)}, u32[]{:S(2)}) copy-start(bf16[2048,2048]{1,0:T(8,128)(2,1)} %param.8) | copy-start | bytes 25165828
  1.6 4.4 %copy-start = (bf16[2048,256]{1,0:T(8,128)(2,1)S(1)}, bf16[2048,256]{1,0:T(8,128)(2,1)}, u32[]{:S(2)}) copy-start(bf16[2048,256]{1,0:T(8,128)(2,1)} %x_ref.1) | copy-start | bytes 3145732
  1.7 23.0 %slice-start = ((s8[8388608]{0:T(1024)(128)(4,1)}), s8[4194304]{0:T(1024)(128)(4,1)S(1)}, s32[]{:S(2)}) async-start(s8[8388608]{0:T(1024)(128)(4,1)} %bitcast.26), calls=%async_computation | async-start | bytes 8388608
  6.0 18.6 %slice-start.1 = ((s8[8388608]{0:T(1024)(128)(4,1)}), s8[4194304]{0:T(1024)(128)(4,1)S(1)}, s32[]{:S(2)}) async-start(s8[8388608]{0:T(1024)(128)(4,1)} %bitcast.26), calls=%async_computation.1 | async-start | bytes 8388608
  7.4 1.0 copy-start.1
  8.3 13.8 %collective-permute-start.3 = (f16[1280,256]{1,0:T(8,128)(2,1)S(1)}, f16[1280,256]{1,0:T(8,128)(2,1)S(1)}, u32[]{:S(2)}, u32[]{:S(2)}) collective-permute-start(f16[1280,256]{1,0:T(8,128)(2,1)S(1)} %pad_maximum_fusion.1), channel_id=1, source_target_pairs={{0,2},{1,5},{2,0},{3,7},{4,6},{5,1},{6,4},{7,3},{8,10},{9,13},{10,... | collective-permute-start | bytes 1966088 | tf_op jit(solution)/shard_map/ppermute | solution.py:109
  10.8 1.2 %copy-start.2 = (bf16[2048,256]{1,0:T(8,128)(2,1)S(1)}, bf16[2048,256]{1,0:T(8,128)(2,1)}, u32[]{:S(2)}) copy-start(bf16[2048,256]{1,0:T(8,128)(2,1)} %copy-done.1) | copy-start | bytes 3145732
  12.8 27.5 %collective-permute-start.1 = (bf16[512,256]{1,0:T(8,128)(2,1)}, bf16[512,256]{1,0:T(8,128)(2,1)S(1)}, u32[]{:S(2)}, u32[]{:S(2)}) collective-permute-start(bf16[512,256]{1,0:T(8,128)(2,1)} %pad_maximum_fusion.2), channel_id=1, source_target_pairs={{0,2},{1,31},{2,4},{3,1},{4,6},{5,3},{6,8},{7,5},{8,10},{9,7},{10,... | collective-permute-start | bytes 786440 | tf_op jit(solution)/shard_map/ppermute | solution.py:197
  22.4 7.2 %collective-permute-start.4 = (f16[640,256]{1,0:T(8,128)(2,1)S(1)}, f16[640,256]{1,0:T(8,128)(2,1)S(1)}, u32[]{:S(2)}, u32[]{:S(2)}) collective-permute-start(f16[640,256]{1,0:T(8,128)(2,1)S(1)} %fusion.47), channel_id=1, source_target_pairs={{0,8},{1,3},{2,10},{3,1},{4,12},{5,7},{6,14},{7,5},{8,0},{9,11},{1... | collective-permute-start | bytes 983048 | tf_op jit(solution)/shard_map/ppermute | solution.py:109
  30.4 9.7 %copy-start.6 = (s32[16,3]{0,1:T(4,128)S(1)}, s32[16,3]{0,1:T(4,128)}, u32[]{:S(2)}) copy-start(s32[16,3]{0,1:T(4,128)} %param.6) | copy-start | bytes 580
  30.4 11.5 %collective-permute-start.5 = (f16[320,256]{1,0:T(8,128)(2,1)}, f16[320,256]{1,0:T(8,128)(2,1)S(1)}, u32[]{:S(2)}, u32[]{:S(2)}) collective-permute-start(f16[320,256]{1,0:T(8,128)(2,1)} %add_convert_fusion), channel_id=1, source_target_pairs={{0,4},{1,9},{2,6},{3,11},{4,0},{5,13},{6,2},{7,15},{8,12},{9,1},{1... | collective-permute-start | bytes 491528 | tf_op jit(solution)/shard_map/ppermute | solution.py:109
  40.1 19.6 %collective-permute-start.14 = (f16[512,1024]{1,0:T(8,128)(2,1)}, f16[512,1024]{1,0:T(8,128)(2,1)}, u32[]{:S(2)}, u32[]{:S(2)}) collective-permute-start(f16[512,1024]{1,0:T(8,128)(2,1)} %fusion.20), channel_id=1, source_target_pairs={{0,2},{1,5},{2,0},{3,7},{4,6},{5,1},{6,4},{7,3},{8,10},{9,13},{10,... | collective-permute-start | bytes 3145736 | tf_op jit(solution)/shard_map/ppermute | solution.py:109
  40.2 5.7 %copy-start.5 = (bf16[512,256]{1,0:T(8,128)(2,1)}, bf16[512,256]{1,0:T(8,128)(2,1)S(1)}, u32[]{:S(2)}) copy-start(bf16[512,256]{1,0:T(8,128)(2,1)S(1)} %collective-permute-done.1.fetched_ref) | copy-start | bytes 786436
  40.2 5.6 %collective-permute-start.2 = (bf16[256,256]{1,0:T(8,128)(2,1)S(1)}, bf16[256,256]{1,0:T(8,128)(2,1)}, u32[]{:S(2)}, u32[]{:S(2)}) collective-permute-start(bf16[256,256]{1,0:T(8,128)(2,1)S(1)} %slice.64), channel_id=1, source_target_pairs={{0,1},{1,0},{2,3},{3,2},{4,5},{5,4},{6,7},{7,6},{8,9},{9,8},{10,11... | collective-permute-start | bytes 393224 | tf_op jit(solution)/shard_map/ppermute | solution.py:198
  42.7 9.7 %collective-permute-start.6 = (f16[320,256]{1,0:T(8,128)(2,1)}, f16[320,256]{1,0:T(8,128)(2,1)}, u32[]{:S(2)}, u32[]{:S(2)}) collective-permute-start(f16[320,256]{1,0:T(8,128)(2,1)} %fusion.61), channel_id=1, source_target_pairs={{0,16},{1,17},{2,18},{3,19},{4,20},{5,21},{6,22},{7,23},{8,24},{9,... | collective-permute-start | bytes 491528 | tf_op jit(solution)/shard_map/ppermute | solution.py:109
  53.4 5.4 %collective-permute-start.7 = (f16[320,256]{1,0:T(8,128)(2,1)S(1)}, f16[320,256]{1,0:T(8,128)(2,1)S(1)}, u32[]{:S(2)}, u32[]{:S(2)}) collective-permute-start(f16[320,256]{1,0:T(8,128)(2,1)S(1)} %fusion.52), channel_id=1, source_target_pairs={{0,4},{1,9},{2,6},{3,11},{4,0},{5,13},{6,2},{7,15},{8,12},{9,1},{1... | collective-permute-start | bytes 491528 | tf_op jit(solution)/shard_map/ppermute | solution.py:109
  54.4 5.4 %copy-start.3 = (f32[512,1024]{1,0:T(8,128)S(1)}, f32[512,1024]{1,0:T(8,128)}, u32[]{:S(2)}) copy-start(f32[512,1024]{1,0:T(8,128)} %fusion.6) | copy-start | bytes 6291460
  59.0 7.1 %collective-permute-start.8 = (f16[640,256]{1,0:T(8,128)(2,1)S(1)}, f16[640,256]{1,0:T(8,128)(2,1)S(1)}, u32[]{:S(2)}, u32[]{:S(2)}) collective-permute-start(f16[640,256]{1,0:T(8,128)(2,1)S(1)} %maximum_select_fusion.2), channel_id=1, source_target_pairs={{0,8},{1,3},{2,10},{3,1},{4,12},{5,7},{6,14},{7,5},{8,0},{9,11},{1... | collective-permute-start | bytes 983048 | tf_op jit(solution)/shard_map/ppermute | solution.py:109
  68.1 6.7 %collective-permute-start.15 = (f32[256,256]{1,0:T(8,128)}, f32[256,256]{1,0:T(8,128)}, u32[]{:S(2)}, u32[]{:S(2)}) collective-permute-start(f32[256,256]{1,0:T(8,128)} %constant_dynamic-slice_fusion.1), channel_id=1, source_target_pairs={{0,2},{1,5},{2,0},{3,7},{4,6},{5,1},{6,4},{7,3},{8,10},{9,13},{10,... | collective-permute-start | bytes 786440 | tf_op jit(solution)/shard_map/ppermute | solution.py:109
  76.3 6.6 %collective-permute-start.16 = (f32[128,256]{1,0:T(8,128)}, f32[128,256]{1,0:T(8,128)S(1)}, u32[]{:S(2)}, u32[]{:S(2)}) collective-permute-start(f32[128,256]{1,0:T(8,128)} %dynamic-slice_add_fusion), channel_id=1, source_target_pairs={{0,4},{1,3},{2,6},{3,1},{4,0},{5,7},{6,2},{7,5},{8,12},{9,11},{10,... | collective-permute-start | bytes 393224 | tf_op jit(solution)/shard_map/ppermute | solution.py:109
  77.2 14.7 %collective-permute-start.9 = (f16[1280,256]{1,0:T(8,128)(2,1)S(1)}, f16[1280,256]{1,0:T(8,128)(2,1)}, u32[]{:S(2)}, u32[]{:S(2)}) collective-permute-start(f16[1280,256]{1,0:T(8,128)(2,1)S(1)} %maximum_select_fusion), channel_id=1, source_target_pairs={{0,2},{1,5},{2,0},{3,7},{4,6},{5,1},{6,4},{7,3},{8,10},{9,13},{10,... | collective-permute-start | bytes 1966088 | tf_op jit(solution)/shard_map/ppermute | solution.py:109
  83.8 9.2 %copy-start.4 = (f32[2048,256]{1,0:T(8,128)S(1)}, f32[2048,256]{1,0:T(8,128)}, u32[]{:S(2)}) copy-start(f32[2048,256]{1,0:T(8,128)} %get-tuple-element.29) | copy-start | bytes 6291460
  83.8 6.2 %collective-permute-start.17 = (f32[128,256]{1,0:T(8,128)S(1)}, f32[128,256]{1,0:T(8,128)S(1)}, u32[]{:S(2)}, u32[]{:S(2)}) collective-permute-start(f32[128,256]{1,0:T(8,128)S(1)} %add_add_fusion), channel_id=1, source_target_pairs={{0,8},{1,17},{2,10},{3,19},{4,12},{5,21},{6,14},{7,23},{8,0},{9,25... | collective-permute-start | bytes 393224 | tf_op jit(solution)/shard_map/ppermute | solution.py:109
  90.1 9.9 %collective-permute-start.18 = (f32[128,256]{1,0:T(8,128)S(1)}, f32[128,256]{1,0:T(8,128)S(1)}, u32[]{:S(2)}, u32[]{:S(2)}) collective-permute-start(f32[128,256]{1,0:T(8,128)S(1)} %add.205), channel_id=1, source_target_pairs={{0,16},{1,9},{2,18},{3,11},{4,20},{5,13},{6,22},{7,15},{8,24},{9,1... | collective-permute-start | bytes 393224 | tf_op jit(solution)/shard_map/ppermute | solution.py:109
  97.8 14.8 %collective-permute-start.12 = (bf16[1024,256]{1,0:T(8,128)(2,1)S(1)}, bf16[1024,256]{1,0:T(8,128)(2,1)S(1)}, u32[]{:S(2)}, u32[]{:S(2)}) collective-permute-start(bf16[1024,256]{1,0:T(8,128)(2,1)S(1)} %get-tuple-element.39), channel_id=1, source_target_pairs={{0,1},{1,0},{2,3},{3,2},{4,5},{5,4},{6,7},{7,6},{8,9},{9,8},{10,11... | collective-permute-start | bytes 1572872 | tf_op jit(solution)/shard_map/ppermute | solution.py:255
  99.5 13.8 %collective-permute-start.10 = (bf16[1024,256]{1,0:T(8,128)(2,1)S(1)}, bf16[1024,256]{1,0:T(8,128)(2,1)S(1)}, u32[]{:S(2)}, u32[]{:S(2)}) collective-permute-start(bf16[1024,256]{1,0:T(8,128)(2,1)S(1)} %get-tuple-element.36), channel_id=1, source_target_pairs={{0,1},{1,0},{2,3},{3,2},{4,5},{5,4},{6,7},{7,6},{8,9},{9,8},{10,11... | collective-permute-start | bytes 1572872 | tf_op jit(solution)/shard_map/ppermute | solution.py:255
  100.1 5.0 %collective-permute-start.19 = (f32[128,256]{1,0:T(8,128)S(1)}, f32[128,256]{1,0:T(8,128)S(1)}, u32[]{:S(2)}, u32[]{:S(2)}) collective-permute-start(f32[128,256]{1,0:T(8,128)S(1)} %add.206), channel_id=1, source_target_pairs={{0,4},{1,3},{2,6},{3,1},{4,0},{5,7},{6,2},{7,5},{8,12},{9,11},{10,... | collective-permute-start | bytes 393224 | tf_op jit(solution)/shard_map/ppermute | solution.py:109
  101.1 11.8 %collective-permute-start.13 = (bf16[1024,256]{1,0:T(8,128)(2,1)S(1)}, bf16[1024,256]{1,0:T(8,128)(2,1)S(1)}, u32[]{:S(2)}, u32[]{:S(2)}) collective-permute-start(bf16[1024,256]{1,0:T(8,128)(2,1)S(1)} %get-tuple-element.40), channel_id=1, source_target_pairs={{0,1},{1,0},{2,3},{3,2},{4,5},{5,4},{6,7},{7,6},{8,9},{9,8},{10,11... | collective-permute-start | bytes 1572872 | tf_op jit(solution)/shard_map/ppermute | solution.py:255
  102.8 10.7 %collective-permute-start.11 = (bf16[1024,256]{1,0:T(8,128)(2,1)S(1)}, bf16[1024,256]{1,0:T(8,128)(2,1)S(1)}, u32[]{:S(2)}, u32[]{:S(2)}) collective-permute-start(bf16[1024,256]{1,0:T(8,128)(2,1)S(1)} %get-tuple-element.37), channel_id=1, source_target_pairs={{0,1},{1,0},{2,3},{3,2},{4,5},{5,4},{6,7},{7,6},{8,9},{9,8},{10,11... | collective-permute-start | bytes 1572872 | tf_op jit(solution)/shard_map/ppermute | solution.py:255
  105.1 6.7 %collective-permute-start.20 = (f32[256,256]{1,0:T(8,128)S(1)}, f32[256,256]{1,0:T(8,128)S(1)}, u32[]{:S(2)}, u32[]{:S(2)}) collective-permute-start(f32[256,256]{1,0:T(8,128)S(1)} %maximum_select_fusion.3), channel_id=1, source_target_pairs={{0,2},{1,5},{2,0},{3,7},{4,6},{5,1},{6,4},{7,3},{8,10},{9,13},{10,... | collective-permute-start | bytes 786440 | tf_op jit(solution)/shard_map/ppermute | solution.py:109
